TPU v7x, 32 devices: a whole 2x2x4 slice. The times are simulated.
32 devices in a mesh: dp: 8 (over z, y), tp: 4 (over x, core).
Axes of the slice: x: 2, y: 2, z: 4, core: 2. Of those that a mesh axis runs over, the one named last changes fastest.
Arguments:
- frames: bfloat16 [16, 2304, 384], P('dp', 'tp'), may hold values from -6 to 6
- targets: bfloat16 [16, 2304, 384], P('dp', 'tp'), may hold values from -6 to 6
- presence: int32 [16, 4], P('dp'), may hold values 0 or 1
- order: int32 [8, 2], P('dp'), may hold values from 0 to 1, each once within a row
- attn_proj: float32 [3, 384, 384], P(None, None, 'tp'), may hold values from -0.3125 to 0.3125
- out_proj: float32 [384, 384], P('tp'), may hold values from -7 to 7
- up_proj: float32 [384, 1536], P(None, 'tp'), may hold values from -0.3125 to 0.3125
- up_bias: float32 [1536], P('tp'), may hold values from -3 to 3
- down_proj: float32 [384, 1536], P(None, 'tp'), may hold values from -0.15625 to 0.15625
- head_proj: float32 [384, 384], replicated, may hold values from -0.3125 to 0.3125
- vectors: float32 [9, 384], replicated
- momentum_attn: float32 [3, 384, 384], P(None, None, 'tp'), may hold values from -256 to 256
- momentum_out: float32 [384, 384], P('tp'), may hold values from -3 to 3
- momentum_up: float32 [384, 1536], P(None, 'tp'), may hold values from -3 to 3
- momentum_bias: float32 [1536], P('tp'), may hold values from -3 to 3
- momentum_down: float32 [384, 1536], P(None, 'tp'), may hold values from -3 to 3
- momentum_head: float32 [384, 384], replicated, may hold values from -224 to 224
- momentum_vectors: float32 [9, 384], replicated, may hold values from -3 to 3
- average_attn: float32 [3, 384, 384], P(None, None, 'tp'), may hold values from -0.3125 to 0.3125
- average_out: float32 [384, 384], P('tp'), may hold values from -7 to 7
- average_up: float32 [384, 1536], P(None, 'tp'), may hold values from -0.3125 to 0.3125
- average_bias: float32 [1536], P('tp'), may hold values from -3 to 3
- average_down: float32 [384, 1536], P(None, 'tp'), may hold values from -0.15625 to 0.15625
- average_head: float32 [384, 384], replicated, may hold values from -0.3125 to 0.3125
- average_vectors: float32 [9, 384], replicated
Outputs:
- loss: float32 [], replicated
- new_attn: float32 [3, 384, 384], P(None, None, 'tp')
- new_out: float32 [384, 384], P('tp')
- new_up: float32 [384, 1536], P(None, 'tp')
- new_bias: float32 [1536], P('tp')
- new_down: float32 [384, 1536], P(None, 'tp')
- new_head: float32 [384, 384], replicated
- new_vectors: float32 [9, 384], replicated
- moment_attn: float32 [3, 384, 384], P(None, None, 'tp')
- moment_out: float32 [384, 384], P('tp')
- moment_up: float32 [384, 1536], P(None, 'tp')
- moment_bias: float32 [1536], P('tp')
- moment_down: float32 [384, 1536], P(None, 'tp')
- moment_head: float32 [384, 384], replicated
- moment_vectors: float32 [9, 384], replicated
- mean_attn: float32 [3, 384, 384], P(None, None, 'tp')
- mean_out: float32 [384, 384], P('tp')
- mean_up: float32 [384, 1536], P(None, 'tp')
- mean_bias: float32 [1536], P('tp')
- mean_down: float32 [384, 1536], P(None, 'tp')
- mean_head: float32 [384, 384], replicated
- mean_vectors: float32 [9, 384], replicated
- grad_frames: float32 [16, 2304, 384], P('dp', 'tp')
Inputs may be any that keep to these rules, and one draw needn't show every extreme that they name: `order`: each row holds every number below 2 once.
All inputs are finite; a program needn't handle non-finite values. No bound on the sum of `presence` on one device may be relied on, other than what follows from the above.
Results may differ from a plain program's by a relative error of at most 0.0095.
Values may be sent and summed in bfloat16 or wider, within the bound.
No kernel may reach another device: no remote copies, remote signals or barrier semaphores. Data moves between devices by JAX's collectives and lax.ppermute only.
A program may use at most 192 MiB of HBM per device.

v0:
```python
import functools
import math

import jax
import jax.numpy as jnp
from jax import lax
from jax.experimental import pallas as pl
from jax.experimental.pallas import tpu as pltpu
from jax.sharding import PartitionSpec as P

CHN = 96
HDIM = 48
HPAD = 64
HEAD = 384


EPSILON = 1e-05
MOMENTUM_RATE = 0.9
LEARN_RATE = 0.02
AVERAGE_RATE = 0.9
SCALE = HDIM ** (-0.5)
LOG_SCALE = SCALE * math.log2(math.e)
GELU_A = math.sqrt(2.0 / math.pi)
GELU_B = 0.044715
SMALL = 16
BLOCK = 384
ROWS = 64
CHUNKS = 3

bf16 = jnp.bfloat16
f32 = jnp.float32
HBM = pl.BlockSpec(memory_space=pltpu.HBM)
SMEM = pl.BlockSpec(memory_space=pltpu.SMEM)
VMEM = pl.BlockSpec(memory_space=pltpu.VMEM)


def kernel_call(body, outs, inputs, limit, micros, name, in_specs=None, out_specs=None, scratch=(), aliases=None):
    return pl.pallas_call(
        body,
        out_shape=outs,
        in_specs=in_specs or [VMEM] * len(inputs),
        out_specs=out_specs or jax.tree.map(lambda _: VMEM, outs),
        scratch_shapes=list(scratch),
        input_output_aliases=aliases or {},
        compiler_params=pltpu.CompilerParams(vmem_limit_bytes=limit << 20),
        cost_estimate=pl.CostEstimate(flops=int(micros * 1e9), bytes_accessed=0, transcendentals=0),
        name=name,
    )(*inputs)


def struct(rows, columns, dtype):
    return jax.ShapeDtypeStruct((rows, columns), dtype)


def contract(left, right, left_dim, right_dim):
    return lax.dot_general(
        left, right, (((left_dim,), (right_dim,)), ((), ())), preferred_element_type=f32
    )


def row_mean(values):
    return jnp.mean(values, axis=-1, keepdims=True)


def column_sum(values):
    return jnp.sum(values, axis=0, keepdims=True)


def normalise(values):
    centred = values - row_mean(values)
    inverse = lax.rsqrt(row_mean(centred * centred) + EPSILON)
    return centred * inverse, inverse


def aligned(index, size):
    return pl.ds(pl.multiple_of(index * size, size), size)


def forward_body(first, heads, query, key, value, *refs):
    mixed, totals, weights, slots, sems = refs[-5:]

    def out_copy(h):
        slot = lax.rem(h, 2)
        return pltpu.make_async_copy(slots.at[slot], weights.at[h + first], sems.at[slot])

    def head(h, carry):
        @pl.when(h >= 2)
        def _():
            out_copy(h - 2).wait()

        rows = aligned(h, HDIM)
        scores = contract(query[rows], key[rows], 0, 0)
        maximum = jnp.max(scores, axis=1, keepdims=True)
        exponent = jnp.exp2((scores - maximum) * LOG_SCALE).astype(bf16)
        slots[lax.rem(h, 2)] = exponent
        out_copy(h).start()
        summed = contract(value[aligned(h, HPAD)], exponent, 1, 1)
        total = summed[HDIM : HDIM + 1]
        mixed[rows] = (summed[:HDIM] / total).astype(bf16)
        totals[pl.ds(h, 1)] = total
        return carry

    lax.fori_loop(0, heads, head, 0)
    for h in range(max(0, heads - 2), heads):
        out_copy(h).wait()


def attention_forward(query, key, value, weights=None):
    heads = query.shape[0] // HDIM
    first = 0 if weights is None else heads
    rows, length = query.shape[1], key.shape[1]
    return kernel_call(
        functools.partial(forward_body, first, heads),
        [
            struct(heads * HDIM, rows, bf16),
            struct(heads, rows, f32),
            jax.ShapeDtypeStruct((2 * heads, rows, length), bf16),
        ],
        (query, key, value) if weights is None else (query, key, value, weights),
        FORWARD_LIMIT,
        4 * heads,
        "attention_forward",
        in_specs=[VMEM] * 3 if weights is None else [VMEM] * 3 + [HBM],
        aliases={} if weights is None else {3: 2},
        out_specs=[VMEM, VMEM, HBM],
        scratch=[pltpu.VMEM((2, rows, length), bf16), pltpu.SemaphoreType.DMA((2,))],
    )


def backward_body(
    first, base, heads, query, key, value, mixed, grad_mixed, totals, weights,
    grad_query, grad_key, grad_value, slots, sums, scaled_all, sems
):
    def in_copy(h):
        slot = lax.rem(h, 2)
        return pltpu.make_async_copy(weights.at[h + base], slots.at[slot], sems.at[slot])

    in_copy(0).start()
    width = key.shape[1] // CHUNKS

    def head(h, carry):
        @pl.when(h + 1 < heads)
        def _():
            in_copy(h + 1).start()

        rows, here = aligned(h + first, HDIM), aligned(h, HDIM)
        inverse = 1.0 / totals[pl.ds(h + first, 1)]
        grad = grad_mixed[rows].astype(f32)
        delta = column_sum(grad * mixed[rows].astype(f32))
        scaled = (grad * inverse).astype(bf16)
        offset = -delta * inverse
        high = offset.astype(bf16).astype(f32)
        row = lax.broadcasted_iota(jnp.int32, (HPAD - HDIM, offset.shape[1]), 0)
        extra = jnp.where(row == 0, high, jnp.where(row == 1, offset - high, 0.0)).astype(bf16)
        scaled_all[...] = jnp.concatenate([scaled, extra], axis=0)
        sums[...] = jnp.zeros_like(sums)
        in_copy(h).wait()

        def chunk(i, carry):
            part = aligned(i, width)
            grad_weights = contract(scaled_all[...], value[aligned(h + first, HPAD), part], 0, 0)
            kept = slots[lax.rem(h, 2), :, part]
            grad_scores = (kept.astype(f32) * grad_weights).astype(bf16)
            sums[...] += contract(key[rows, part], grad_scores, 1, 1)
            grad_key[here, part] = (contract(query[rows], grad_scores, 1, 0) * SCALE).astype(bf16)
            grad_value[here, part] = contract(scaled_all[:HDIM], kept, 1, 0).astype(bf16)
            return carry

        lax.fori_loop(0, CHUNKS, chunk, 0)
        grad_query[here] = (sums[...] * SCALE).astype(bf16)
        return carry

    lax.fori_loop(0, heads, head, 0)


def attention_backward(first, base, heads, query, key, value, mixed, grad_mixed, totals, weights):
    rows, length = query.shape[1], key.shape[1]
    return kernel_call(
        functools.partial(backward_body, first, base, heads),
        [
            struct(heads * HDIM, rows, bf16),
            struct(heads * HDIM, length, bf16),
            struct(heads * HDIM, length, bf16),
        ],
        (query, key, value, mixed, grad_mixed, totals, weights),
        BACKWARD_LIMIT,
        5.5 * heads,
        "attention_backward",
        in_specs=[VMEM] * 6 + [HBM],
        scratch=[
            pltpu.VMEM((2, rows, length), bf16),
            pltpu.VMEM((HDIM, rows), f32),
            pltpu.VMEM((HPAD, rows), bf16),
            pltpu.SemaphoreType.DMA((2,)),
        ],
    )


def take_body(place, stacked, taken):
    taken[...] = stacked[place[0]]


def take(stacked, place):
    count, rows, columns = stacked.shape
    return kernel_call(
        take_body, struct(rows, columns, stacked.dtype), (place, stacked), 2, 1, "take", in_specs=[SMEM, VMEM]
    )


def pack_body(place, attn, out, up, down, bias, targets, attn_low, sent, goal):
    share, deep = out.shape[0], up.shape[0]
    base = share + 2 * deep
    goal[...] = targets[place[0]]
    attn_low[...] = attn[...].astype(bf16)
    sent[:share] = out[...].astype(bf16)
    sent[share : share + deep] = up[...].astype(bf16)
    sent[share + deep : base] = down[...].astype(bf16)
    high = bias[...].astype(bf16)
    low = (bias[...] - high.astype(f32)).astype(bf16)
    zeros = jnp.zeros((SMALL - 2, bias.shape[1]), bf16)
    sent[base : base + SMALL] = jnp.concatenate([high, low, zeros], axis=0)


def pack(place, attn, out, up, down, bias, targets):
    rows = out.shape[0] + 2 * up.shape[0] + SMALL
    return kernel_call(
        pack_body,
        [struct(attn.shape[0], HEAD, bf16), struct(rows, HEAD, bf16), struct(targets.shape[1], HEAD, bf16)],
        (place, attn, out, up, down, bias, targets),
        8,
        PACK_MICROS,
        "pack",
        in_specs=[SMEM] + [VMEM] * 6,
    )


def weight_rows(left, right):
    share = left.shape[0] // 3
    return jnp.concatenate(
        [block[m * share : (m + 1) * share] for m in range(3) for block in (left, right)], axis=0
    )


def project_into(normed, left, right, query, key, value):
    weights = weight_rows(left[...], right[...])
    size = weights.shape[0] // 3
    rows = query.shape[1]
    query[...] = contract(weights[:size], normed[:rows], 1, 1).astype(bf16)
    both = contract(weights[size:], normed, 1, 1).astype(bf16)
    key[...] = both[:size]
    row = lax.broadcasted_iota(jnp.int32, (HPAD - HDIM, normed.shape[0]), 0)
    ends = jnp.where(row < 2, 1.0, 0.0).astype(bf16)
    for h in range(size // HDIM):
        value[h * HPAD : h * HPAD + HDIM] = both[size + h * HDIM : size + (h + 1) * HDIM]
        value[h * HPAD + HDIM : (h + 1) * HPAD] = ends


def project_near_body(
    place, frames, got, frames_other, got_other, vectors, left, right, query, key, value, first, every
):
    quarter = got.shape[0]
    for j, source in enumerate((frames, got, frames_other, got_other)):
        part = source[place[0]] if j % 2 == 0 else source[...]
        rows = slice(j * quarter, (j + 1) * quarter)
        every[rows] = part
        first[rows] = (normalise(part.astype(f32))[0] * vectors[0:1] + vectors[1:2]).astype(bf16)
    project_into(first[...], left, right, query, key, value)


def projected(rows, length, size):
    return [
        struct(size, rows, bf16),
        struct(size, length, bf16),
        struct(size // HDIM * HPAD, length, bf16),
    ]


def project_near(place, frames, got, frames_other, got_other, vectors, left, right):
    quarter, model = got.shape
    size = 2 * left.shape[0] // 3
    return kernel_call(
        project_near_body,
        projected(2 * quarter, 4 * quarter, size) + [struct(4 * quarter, model, bf16)] * 2,
        (place, frames, got, frames_other, got_other, vectors, left, right),
        16,
        4,
        "project_near",
        in_specs=[SMEM] + [VMEM] * 7,
    )


def project_far_body(first, *refs):
    project_into(first[...], *refs)


def project_far(first, left, right):
    length = first.shape[0]
    size = 2 * left.shape[0] // 3
    return kernel_call(
        project_far_body,
        projected(length // 2, length, size),
        (first, left, right),
        12,
        3,
        "project_far",
    )


def by_rows(function, *values):
    pieces = [
        function(*(v[start : start + ROWS] for v in values)) for start in range(0, values[0].shape[0], ROWS)
    ]
    return [jnp.concatenate(parts, axis=0) for parts in zip(*pieces)]


def middle_body(
    place, attended_near, attended_far, frames, targets, goal_got, keep, vectors, head, *refs
):
    blocks = refs[:4]
    grad_middle_out, grad_near, grad_far, kept_out, sent_out, small_out = refs[4:10]
    second_all, ffn_all, final_all, pred_all, attn_all, hidden_all, pre_all, goal, bias_sums = refs[10:]
    rows = grad_middle_out.shape[0]
    quarter = targets.shape[1]
    deep = head.shape[0]
    share = grad_near.shape[0] // 2
    base = share + 2 * deep
    half = 2 * share
    goal[:quarter] = targets[place[1]]
    goal[quarter:] = goal_got[...]
    gain, shift = vectors[4:5], vectors[5:6]
    scale_one, scale_two = vectors[3:4], vectors[7:8]
    out_low = jnp.concatenate([b[:share] for b in blocks], axis=0)
    head_low = head[...].astype(bf16)
    small_out[...] = jnp.zeros_like(small_out)
    bias_sums[...] = jnp.zeros_like(bias_sums)

    def block_step(step, carry):
        here = aligned(step, BLOCK)

        def add(row, values):
            small_out[row : row + 1] += column_sum(values)

        mixed = contract(attended_near[:, here], out_low[:half], 0, 0) + contract(
            attended_far[:, here], out_low[half:], 0, 0
        )

        def first_norm(mixed, frames):
            biased = mixed + vectors[2:3]
            middle = frames.astype(f32) + scale_one * biased
            normed, inverse = normalise(middle)
            return biased, middle, normed, inverse, (normed * gain + shift).astype(bf16)

        biased_one, middle, normed, inverse, second = by_rows(first_norm, mixed, frames[here])
        second_all[here] = second
        slopes = []
        mixed = None
        for j, block in enumerate(blocks):
            parts = block[base : base + SMALL].astype(f32)
            bias = parts[0:1] + parts[1:2]

            def gelu(pre):
                pre = pre + bias
                square = pre * pre
                tanh = jnp.tanh(pre * (GELU_A + (GELU_A * GELU_B) * square))
                phi = 0.5 + 0.5 * tanh
                curve = (1.0 - tanh * tanh) * (0.5 * GELU_A + (1.5 * GELU_A * GELU_B) * square)
                return (pre * phi).astype(bf16), phi + pre * curve

            hidden, slope = by_rows(gelu, contract(second, block[share : share + deep], 1, 0))
            hidden_all[j, here] = hidden
            slopes.append(slope)
            part = contract(hidden, block[share + deep : base], 1, 1)
            mixed = part if j == 0 else mixed + part

        def second_scale(mixed, middle):
            biased = mixed + vectors[6:7]
            return biased, (middle + scale_two * biased).astype(bf16)

        biased_two, final = by_rows(second_scale, mixed, middle)
        final_all[here] = final

        def error(pred, goal):
            diff = pred + vectors[8:9] - goal.astype(f32)
            smooth = jnp.sqrt(diff * diff + 1.0)
            add(7, keep[...] * (smooth - 1.0) / HEAD)
            grad = (keep[...] * (diff / smooth) / HEAD).astype(bf16)
            add(6, grad.astype(f32))
            return (grad,)

        (grad_pred,) = by_rows(error, contract(final, head_low, 1, 0), goal[here])
        pred_all[here] = grad_pred

        grad_final = contract(grad_pred, head_low, 1, 1)

        def scale_back(grad, biased):
            ffn = grad * scale_two
            add(4, ffn)
            add(5, grad * biased)
            return (ffn.astype(bf16),)

        (ffn_low,) = by_rows(scale_back, grad_final, biased_two)
        ffn_all[here] = ffn_low
        grad_second = None
        for j, block in enumerate(blocks):

            def gelu_back(grad, slope):
                low = (grad * slope).astype(bf16)
                bias_sums[j : j + 1] += column_sum(low.astype(f32))
                return (low,)

            grad = contract(ffn_low, block[share + deep : base], 1, 0)
            (low,) = by_rows(gelu_back, grad, slopes[j])
            pre_all[j, here] = low
            part = contract(low, block[share : share + deep], 1, 1)
            grad_second = part if j == 0 else grad_second + part

        def norm_back(grad, normed, inverse, grad_final, biased):
            add(2, grad * normed)
            add(3, grad)
            scaled = grad * gain
            back = inverse * (scaled - row_mean(scaled) - normed * row_mean(scaled * normed))
            total = grad_final + back
            attn = total * scale_one
            add(0, attn)
            add(1, total * biased)
            return total, attn.astype(bf16)

        grad_middle, attn_low = by_rows(norm_back, grad_second, normed, inverse, grad_final, biased_one)
        grad_middle_out[here] = grad_middle
        attn_all[here] = attn_low
        grad_near[:, here] = contract(out_low[:half], attn_low, 1, 1).astype(bf16)
        grad_far[:, here] = contract(out_low[half:], attn_low, 1, 1).astype(bf16)
        return carry

    lax.fori_loop(0, rows // BLOCK, block_step, 0)

    attn_low = attn_all[...]
    grad_out = jnp.concatenate(
        [contract(attended_near[...], attn_low, 1, 0), contract(attended_far[...], attn_low, 1, 0)], axis=0
    ).astype(bf16)
    for j in range(4):
        target = (kept_out, sent_out)[j % 2]
        start = (j // 2) * base
        target[start : start + share] = grad_out[j * share : (j + 1) * share]
        small_out[pl.ds(8 + lax.bitwise_xor(place[0], j), 1)] = bias_sums[j : j + 1]

    def weight_step(i, carry):
        for k, target in enumerate((kept_out, sent_out)):
            start = pl.multiple_of(i * base + share, SMALL)
            up = contract(second_all[...], pre_all[2 * i + k], 0, 0).astype(bf16)
            down = contract(ffn_all[...], hidden_all[2 * i + k], 0, 0).astype(bf16)
            target[pl.ds(start, deep)] = up
            target[pl.ds(pl.multiple_of(start + deep, SMALL), deep)] = down
        return carry

    lax.fori_loop(0, 2, weight_step, 0)
    grad_head = contract(final_all[...], pred_all[...], 0, 0).astype(bf16)
    column = lax.broadcasted_iota(jnp.int32, (1, HEAD), 1)
    loss = jnp.sum(small_out[7:8], axis=1, keepdims=True)
    small_out[7:8] = jnp.where(column == 0, loss, 0.0)
    core = lax.rem(place[0], 2)
    size = deep // 2
    for target, first in ((kept_out, core == 0), (sent_out, core == 1)):
        target[2 * base : 2 * base + size] = jnp.where(first, grad_head[:size], grad_head[size:])
        target[2 * base + size :] = jnp.zeros((2 * SMALL, HEAD), bf16)


def middle_step(place, attended_near, attended_far, frames, targets, goal_got, keep, vectors, head, blocks):
    rows, model = frames.shape[0] // 2, frames.shape[1]
    base = blocks[0].shape[0] - SMALL
    count = 2 * base + HEAD // 2 + 2 * SMALL
    inputs = (place, attended_near, attended_far, frames, targets, goal_got, keep, vectors, head, *blocks)
    return kernel_call(
        middle_body,
        [
            struct(rows, model, f32),
            struct(*attended_near.shape, bf16),
            struct(*attended_far.shape, bf16),
            struct(count, HEAD, bf16),
            struct(count, HEAD, bf16),
            struct(SMALL, HEAD, f32),
        ],
        inputs,
        MIDDLE_LIMIT,
        20,
        "middle_step",
        in_specs=[SMEM] + [VMEM] * 12,
        scratch=[
            *[pltpu.VMEM((rows, model), bf16)] * 5,
            pltpu.VMEM((4, rows, HEAD), bf16),
            pltpu.VMEM((4, rows, HEAD), bf16),
            pltpu.VMEM((rows, HEAD), bf16),
            pltpu.VMEM((8, HEAD), f32),
        ],
    )


def fold_body(plan, place, left, right, *targets):
    for target, ranges in zip(targets, plan):
        base = 0
        for start, stop, *choice in ranges:
            if choice:
                size = (stop - start) // 2
                source = pl.ds(pl.multiple_of(start + choice[0](place) * size, SMALL), size)
            else:
                size = stop - start
                source = pl.ds(start, size)
            total = left[source].astype(f32) + right[source].astype(f32)
            target[base : base + size] = total.astype(target.dtype)
            base += size


def fold(left, right, plan, place=None, dtype=bf16):
    shapes = [
        struct(sum((r[1] - r[0]) // (2 if len(r) > 2 else 1) for r in ranges), left.shape[1], dtype)
        for ranges in plan
    ]
    if place is None:
        place = jnp.zeros((1,), jnp.int32)
    return kernel_call(
        functools.partial(fold_body, plan),
        shapes,
        (place, left, right),
        6,
        0.3,
        "fold",
        in_specs=[SMEM, VMEM, VMEM],
    )


def join_body(bit, place, kept, got, both):
    size = kept.shape[0]
    both[pl.ds(pl.multiple_of(bit(place) * size, SMALL), size)] = kept[...]
    both[pl.ds(pl.multiple_of((1 - bit(place)) * size, SMALL), size)] = got[...]


def join(kept, got, bit, place):
    return kernel_call(
        functools.partial(join_body, bit),
        struct(2 * kept.shape[0], kept.shape[1], kept.dtype),
        (place, kept, got),
        6,
        0.3,
        "join",
        in_specs=[SMEM, VMEM, VMEM],
    )


def gather_rows(parts):
    return jnp.concatenate([p[...] for p in parts], axis=0)


def weight_grads(grads, first, kept, sent, base=0):
    queries, keys, values = grads
    rows = queries[0].shape[1]
    query = contract(gather_rows(queries), first[:rows], 1, 0)
    both = contract(gather_rows(keys + values), first[...], 1, 0)
    share = query.shape[0] // 2
    for m in range(3):
        for j, target in enumerate((kept, sent)):
            start = (max(m - 1, 0) * 2 + j) * share
            part = (query if m == 0 else both)[start : start + share]
            target[m * share : (m + 1) * share] = part.astype(bf16)


def far_grads_body(calls, first, *refs):
    grads = [refs[k * calls : (k + 1) * calls] for k in range(3)]
    weight_grads(grads, first[...], *refs[3 * calls :])


def far_grads(grads, first):
    queries, keys, values = zip(*grads)
    count = 3 * sum(q.shape[0] for q in queries) // 2
    return kernel_call(
        functools.partial(far_grads_body, len(grads)),
        [struct(count, HEAD, bf16)] * 2,
        (first, *queries, *keys, *values),
        12,
        4,
        "far_grads",
    )


def post_body(calls, near, *refs):
    queries, keys, values = (refs[k * calls : (k + 1) * calls] for k in range(3))
    first, frames, vectors, small_in = refs[3 * calls : 3 * calls + 4]
    blocks = refs[3 * calls + 4 : 3 * calls + 8]
    mine, other, kept, sent, small = refs[3 * calls + 8 :]
    share = blocks[0].shape[0] // 3
    rows = mine.shape[0]

    def rows_of(m):
        return jnp.concatenate([b[m * share : (m + 1) * share] for b in blocks], axis=0)

    weight_grads((queries[:near], keys[:near], values[:near]), first[...], kept, sent)
    both = jnp.concatenate([rows_of(1), rows_of(2)], axis=0)
    query_rows = rows_of(0)
    small[...] = small_in[...]

    def part(step, carry):
        here = aligned(step, BLOCK)
        there = pl.ds(pl.multiple_of(rows + step * BLOCK, BLOCK), BLOCK)

        def pulled(parts, columns, weights):
            return contract(jnp.concatenate([p[:, columns] for p in parts], axis=0), weights, 0, 0)

        def ends(total, place):
            normed = normalise(frames[place].astype(f32))[0]
            small[12:13] += column_sum(total * normed)
            small[13:14] += column_sum(total)

        total = pulled(keys + values, here, both) + pulled(queries, here, query_rows)
        mine[here] = total
        ends(total, here)
        rest = pulled(keys + values, there, both)
        other[here] = rest.astype(bf16)
        ends(rest, there)
        return carry

    lax.fori_loop(0, rows // BLOCK, part, 0)


def post_step(grads, first, frames, vectors, small, blocks):
    length, model = first.shape
    rows = length // 2
    queries, keys, values = zip(*grads)
    payload = struct(blocks[0].shape[0], model, bf16)
    return kernel_call(
        functools.partial(post_body, len(grads), 2),
        [struct(rows, model, f32), struct(rows, model, bf16), payload, payload, struct(*small.shape, f32)],
        (*queries, *keys, *values, first, frames, vectors, small, *blocks),
        POST_LIMIT,
        8,
        "post_step",
    )


def finish_body(mine, got, frames, vectors, grad_middle, own, returned):
    quarter = own.shape[0]
    size = quarter // 3

    def part(step, carry):
        for target, base in ((own, 0), (returned, quarter)):
            there = aligned(step, size)
            here = pl.ds(pl.multiple_of(base + step * size, size), size)
            grad = mine[here] + got[here].astype(f32)
            normed, inverse = normalise(frames[here].astype(f32))
            scaled = grad * vectors[0:1]
            back = inverse * (scaled - row_mean(scaled) - normed * row_mean(scaled * normed))
            target[there] = (grad_middle[here] + back).astype(target.dtype)
        return carry

    lax.fori_loop(0, 3, part, 0)


def finish(mine, got, frames, vectors, grad_middle):
    rows, model = mine.shape
    return kernel_call(
        finish_body,
        [struct(rows // 2, model, f32), struct(rows // 2, model, bf16)],
        (mine, got, frames, vectors, grad_middle),
        16,
        3,
        "finish",
    )


def update(weight, moment, average, grad):
    moment_new = MOMENTUM_RATE * moment + grad
    weight_new = weight - LEARN_RATE * (grad + MOMENTUM_RATE * moment_new)
    average_new = AVERAGE_RATE * average + (1.0 - AVERAGE_RATE) * weight_new
    return (weight_new, moment_new, average_new)


CORE_PAIRS = [(0, 1), (1, 0), (2, 3), (3, 2)]
CHIP_PAIRS = [(0, 2), (2, 0), (1, 3), (3, 1)]
FORWARD_LIMIT = 28
BACKWARD_LIMIT = 28
MIDDLE_LIMIT = 30
POST_LIMIT = 20
PACK_MICROS = 3


def swap_core(values):
    return lax.ppermute(values, "tp", CORE_PAIRS)


def swap_chip(values):
    return lax.ppermute(values, "tp", CHIP_PAIRS)


def swap_dp(values, step, size):
    return lax.ppermute(values, "dp", [(i, i ^ step) for i in range(size)])


def pick(stacked, place):
    return lax.dynamic_index_in_dim(stacked, place, 0, False)


def tie(value, *others):
    return lax.optimization_barrier((value, *others))[0]


def per_device(
    frames,
    targets,
    presence,
    order,
    attn_proj,
    out_proj,
    up_proj,
    up_bias,
    down_proj,
    head_proj,
    vectors,
    momentum_attn,
    momentum_out,
    momentum_up,
    momentum_bias,
    momentum_down,
    momentum_head,
    momentum_vectors,
    average_attn,
    average_out,
    average_up,
    average_bias,
    average_down,
    average_head,
    average_vectors,
):
    size = lax.axis_size("dp")
    place = lax.axis_index("tp")
    chip, core = place // 2, place % 2
    share, deep = out_proj.shape[0], up_proj.shape[0]
    got = swap_chip(take(frames, (1 - chip).reshape(1)))
    frames_other = swap_core(frames)
    attn_own, sent, goal = pack(
        order[0, 1 - chip].reshape(1),
        jnp.swapaxes(attn_proj, 1, 2).reshape(3 * share, HEAD),
        out_proj,
        up_proj,
        down_proj,
        up_bias[None],
        targets,
    )
    attn_core = swap_core(attn_own)
    sent_core = swap_core(sent)
    got_other = swap_core(tie(got, attn_own))
    attn_chip = swap_chip(tie(attn_own, got))
    query, key, value, first, every = project_near(
        chip.reshape(1), frames, got, frames_other, got_other, vectors, attn_own, attn_core
    )
    sent_chip = swap_chip(tie(sent, first))
    near = (query, key, value)
    near_out = attention_forward(*near)
    attn_both = swap_core(tie(attn_chip, first))
    far = project_far(tie(first, near_out[0]), attn_chip, attn_both)
    sent_both = swap_core(tie(sent_chip, far[0]))
    goal_got = swap_chip(tie(goal, far[0]))
    far_out = attention_forward(*far, near_out[2])
    keep = jnp.repeat(pick(presence, chip).astype(f32), CHN)[None, :]
    where = jnp.stack([place, order[0, chip]])
    grad_middle, grad_near, grad_far, kept, sent, small = middle_step(
        where, near_out[0], far_out[0], every, targets, goal_got, keep, vectors, head_proj,
        (sent, sent_core, sent_chip, sent_both),
    )

    inputs = ((*near, near_out[0], grad_near, near_out[1], far_out[2]), (*far, far_out[0], grad_far, *far_out[1:]))
    here = near[0].shape[0] // HDIM

    def backward(part, first_head, heads, *after):
        query, *others = inputs[part]
        return attention_backward(first_head, part * here + first_head, heads, tie(query, *after), *others)

    block = share + 2 * deep
    half = HEAD // 2
    full = block + half + 2 * SMALL
    spot = lax.axis_index("dp").reshape(1)
    bits = [lambda p: p[0] % 2, lambda p: p[0] // 2 % 2]
    others = [lambda p: 1 - p[0] % 2, lambda p: 1 - p[0] // 2 % 2]
    steps = [1 << k for k in range(size.bit_length() - 1)]
    last_rows = (2 * block, full + block)
    rows = 3 * share

    got_core = swap_core(sent)
    kept, sent = fold(
        kept, got_core, [[(0, block), last_rows], [(block, 2 * block), last_rows]]
    )
    got_chip = swap_chip(sent)
    far_all = backward(1, 0, here, sent)
    kept, sent = fold(
        kept, tie(got_chip, far_all[0]), [[(0, full, bits[0])], [(0, full, others[0])]], spot
    )
    got_y = swap_dp(sent, 1, size)
    far_kept, far_sent = far_grads([far_all], tie(first, sent))
    got_far = swap_core(far_sent)
    near_one = backward(0, 0, here // 2, sent, far_sent)
    (far_kept,) = fold(far_kept, tie(got_far, near_one[0]), [[(0, rows)]])
    got_far = swap_chip(far_kept)
    (kept,) = fold(kept, tie(got_y, near_one[0]), [[(0, full // 2)]])
    got_z = swap_dp(kept, 2, size)
    near_two = backward(0, here // 2, here // 2, kept, far_kept)
    (kept,) = fold(kept, tie(got_z, near_two[0]), [[(0, full // 2)]])
    got_step = swap_dp(kept, steps[2], size)
    mine, other, near_kept, near_sent, small = post_step(
        [near_one, near_two, far_all],
        tie(first, kept, got_far),
        every,
        vectors,
        small,
        (attn_own, attn_core, attn_chip, attn_both),
    )
    got_near = swap_core(near_sent)
    got_small = swap_core(small)
    other_rows = swap_core(other)
    (near_kept,) = fold(near_kept, got_far, [[(0, rows)]], dtype=f32)
    (attn_kept,) = fold(near_kept, got_near, [[(0, rows)]])
    got_attn = swap_dp(attn_kept, 1, size)
    (small,) = fold(small, tie(got_small, attn_kept), [[(0, SMALL)]], dtype=f32)
    got_small = swap_chip(small)
    own_rows, returned = finish(mine, other_rows, every, vectors, tie(grad_middle, attn_kept, small))
    returned = swap_chip(returned)
    (small,) = fold(small, tie(got_small, own_rows), [[(0, SMALL)]], dtype=f32)
    def settle(kept, got_kept, returned):
        kept = join(kept, got_kept, bits[0], spot)
        returned = returned.astype(f32)
        grad_frames = jnp.where(
            chip == 0, jnp.stack([own_rows, returned]), jnp.stack([returned, own_rows])
        )
        kept = kept.astype(f32)
        grad_out = kept[:share]
        grad_up = kept[share : share + deep]
        grad_down = kept[share + deep : block]
        head_mine = kept[block : block + half]
        head_other = swap_core(head_mine.astype(bf16)).astype(f32)
        grad_head = jnp.where(
            core == 0,
            jnp.concatenate([head_mine, head_other], axis=0),
            jnp.concatenate([head_other, head_mine], axis=0),
        )
        second_set = update(out_proj, momentum_out, average_out, grad_out)
        third_set = update(up_proj, momentum_up, average_up, grad_up)
        fifth_set = update(down_proj, momentum_down, average_down, grad_down)
        sixth_set = update(head_proj, momentum_head, average_head, grad_head)
        return grad_frames, *second_set, *third_set, *fifth_set, *sixth_set

    for step in steps:
        got_small = swap_dp(small, step, size)
        if step == steps[-1]:
            last = settle(kept, got_kept, returned)
            got_attn = tie(got_attn, *last)
        (attn_kept,) = fold(
            attn_kept, tie(got_attn, small), [[(0, rows)]], dtype=f32 if step == steps[-1] else bf16
        )
        if step < steps[-1]:
            got_attn = swap_dp(attn_kept, 2 * step, size)
        (small,) = fold(small, tie(got_small, attn_kept), [[(0, SMALL)]], dtype=f32)
        if step == 1:
            for high in steps[2:]:
                got_step = tie(got_step, small) if high == steps[2] else swap_dp(kept, high, size)
                (kept,) = fold(kept, got_step, [[(0, full // 2)]])
            got_kept = swap_dp(kept, 1, size)
        elif step == 2:
            returned = tie(returned, attn_kept)
    grad_frames, *sets = last
    second_set, third_set, fifth_set, sixth_set = (sets[k : k + 3] for k in range(0, 12, 3))
    grad_attn_proj = jnp.swapaxes(attn_kept.reshape(3, share, HEAD), 1, 2)
    loss = small[7, 0]
    grad_up_bias = pick(small[8:12], place)
    grad_vectors = jnp.concatenate([small[12:14], small[:7]], axis=0)
    first_set = update(attn_proj, momentum_attn, average_attn, grad_attn_proj)
    fourth_set = update(up_bias, momentum_bias, average_bias, grad_up_bias)
    seventh_set = update(vectors, momentum_vectors, average_vectors, grad_vectors)
    return (
        loss,
        first_set[0],
        second_set[0],
        third_set[0],
        fourth_set[0],
        fifth_set[0],
        sixth_set[0],
        seventh_set[0],
        first_set[1],
        second_set[1],
        third_set[1],
        fourth_set[1],
        fifth_set[1],
        sixth_set[1],
        seventh_set[1],
        first_set[2],
        second_set[2],
        third_set[2],
        fourth_set[2],
        fifth_set[2],
        sixth_set[2],
        seventh_set[2],
        grad_frames,
    )


def solution(mesh):
    in_specs = (
        P("dp", "tp", None),
        P("dp", "tp", None),
        P("dp", None),
        P("dp", None),
        P(None, None, "tp"),
        P("tp", None),
        P(None, "tp"),
        P("tp"),
        P(None, "tp"),
        P(),
        P(),
        P(None, None, "tp"),
        P("tp", None),
        P(None, "tp"),
        P("tp"),
        P(None, "tp"),
        P(),
        P(),
        P(None, None, "tp"),
        P("tp", None),
        P(None, "tp"),
        P("tp"),
        P(None, "tp"),
        P(),
        P(),
    )
    out_specs = (
        P(),
        P(None, None, "tp"),
        P("tp", None),
        P(None, "tp"),
        P("tp"),
        P(None, "tp"),
        P(),
        P(),
        P(None, None, "tp"),
        P("tp", None),
        P(None, "tp"),
        P("tp"),
        P(None, "tp"),
        P(),
        P(),
        P(None, None, "tp"),
        P("tp", None),
        P(None, "tp"),
        P("tp"),
        P(None, "tp"),
        P(),
        P(),
        P("dp", "tp", None),
    )
    return jax.shard_map(
        per_device, mesh=mesh, in_specs=in_specs, out_specs=out_specs, check_vma=False
    )
```

profile of v0, /device:TPU:0, one launch (start us, length us, event | category | flops | bytes accessed | tf_op | source)
XLA Modules:
  0.0 205.6 jit_solution(14269340548422537242)
XLA Ops:
  0.8 2.1 %take.1 = bf16[576,384]{1,0:T(8,128)(2,1)} custom-call(s32[1]{0:T(128)} %bitcast.1.place, bf16[2,576,384]{2,1,0:T(8,128)(2,1)} %frames.1), custom_call_target="tpu_custom_call" | custom-call | flops 1000000000 | tf_op jit(solution)/shard_map/take/pallas_call | solution.py:38
  2.9 2.9 %collective-permute-start = (bf16[576,384]{1,0:T(8,128)(2,1)}, bf16[576,384]{1,0:T(8,128)(2,1)}, u32[]{:S(2)}, u32[]{:S(2)}) collective-permute-start(bf16[576,384]{1,0:T(8,128)(2,1)} %take.1), channel_id=1, source_target_pairs={{0,2},{2,0},{1,3},{3,1},{4,6},{6,4},{5,7},{7,5},{8,10},{10,8},{9,1... | collective-permute-start | bytes 1327112 | tf_op jit(solution)/shard_map/ppermute | solution.py:689
  6.5 1.7 pack.1
  8.2 8.1 %collective-permute-done.got = bf16[576,384]{1,0:T(8,128)(2,1)} collective-permute-done((bf16[576,384]{1,0:T(8,128)(2,1)}, bf16[576,384]{1,0:T(8,128)(2,1)}, u32[]{:S(2)}, u32[]{:S(2)}) %collective-permute-start) | collective-permute-done | bytes 442400 | tf_op jit(solution)/shard_map/ppermute | solution.py:689
  17.7 1.7 collective-permute-start.4
  20.9 1.0 copy-done.22
  21.9 0.9 copy-done.26
  22.9 3.7 %project_near.1 = (bf16[192,1152]{1,0:T(8,128)(2,1)S(1)}, bf16[192,2304]{1,0:T(8,128)(2,1)S(1)}, bf16[256,2304]{1,0:T(8,128)(2,1)S(1)}, bf16[2304,384]{1,0:T(8,128)(2,1)S(1)}, bf16[2304,384]{1,0:T(8,128)(2,1)S(1)}) custom-call(s32[1]{0:T(128)} %bitcast.place, bf16[2,576,384]{2,1,0:T(8,128)(2,1)} %frames.1, bf16[576,384]{1,0:T(8,128)(2,1)} %collective-permute-done.got, ...), custom_call_target="tpu_custom_call" | custom-call | flops 4000000000 | tf_op jit(solution)/shard_map/project_near/pallas_call | solution.py:38
  27.6 0.8 collective-permute-start.8
  28.3 15.8 %attention_forward.2 = (bf16[192,1152]{1,0:T(8,128)(2,1)S(1)}, f32[4,1152]{1,0:T(4,128)S(1)}, bf16[8,1152,2304]{2,1,0:T(8,128)(2,1)}) custom-call(bf16[192,1152]{1,0:T(8,128)(2,1)S(1)} %get-tuple-element.140.query, bf16[192,2304]{1,0:T(8,128)(2,1)S(1)} %get-tuple-element.99.key, bf16[256,2304]{1,0:T(8,128)(2,1)S(1)} %get-tuple-element.100.value), custom_call_target="tpu_custom_call" | custom-call | flops 16000000000 | tf_op jit(solution)/shard_map/attention_forward/pallas_call | solution.py:38
  44.2 1.4 project_far.1
  45.7 1.3 collective-permute-start.6
  47.1 15.8 %attention_forward.3 = (bf16[192,1152]{1,0:T(8,128)(2,1)S(1)}, f32[4,1152]{1,0:T(4,128)S(1)}, bf16[8,1152,2304]{2,1,0:T(8,128)(2,1)}) custom-call(bf16[192,1152]{1,0:T(8,128)(2,1)S(1)} %get-tuple-element.121.query, bf16[192,2304]{1,0:T(8,128)(2,1)S(1)} %get-tuple-element.107.key, ...), custom_call_target="tpu_custom_call", output_to_operand_aliasing={{2}: (3, {})} | custom-call | flops 16000000000 | tf_op jit(solution)/shard_map/attention_forward/pallas_call | solution.py:38
  63.0 26.2 %middle_step.1 = (f32[1152,384]{1,0:T(8,128)S(1)}, bf16[192,1152]{1,0:T(8,128)(2,1)S(1)}, bf16[192,1152]{1,0:T(8,128)(2,1)S(1)}, bf16[1952,384]{1,0:T(8,128)(2,1...) custom-call(s32[2]{0:T(128)S(1)} %pad_add_fusion.place, ...), custom_call_target="tpu_custom_call" | custom-call | flops 20000000000 | tf_op jit(solution)/shard_map/middle_step/pallas_call | solution.py:38
  89.3 1.1 copy-done
  90.4 1.2 copy-done.34
  91.6 0.8 copy-done.46
  93.5 3.3 %collective-permute-done.10.right = bf16[1952,384]{1,0:T(8,128)(2,1)} collective-permute-done((bf16[1952,384]{1,0:T(8,128)(2,1)}, bf16[1952,384]{1,0:T(8,128)(2,1)}, u32[]{:S(2)}, u32[]{:S(2)}) %collective-permute-start.10) | collective-permute-done | bytes 1499168 | tf_op jit(solution)/shard_map/ppermute | solution.py:685
  96.7 1.4 copy-done.1
  98.1 1.9 fold.16
  100.1 0.9 collective-permute-start.11
  101.0 1.0 copy-done.47
  102.0 22.1 %attention_backward.3 = (bf16[192,1152]{1,0:T(8,128)(2,1)S(1)}, bf16[192,2304]{1,0:T(8,128)(2,1)S(1)}, bf16[192,2304]{1,0:T(8,128)(2,1)S(1)}) custom-call(bf16[192,1152]{1,0:T(8,128)(2,1)S(1)} %copy-done.43, bf16[192,2304]{1,0:T(8,128)(2,1)S(1)} %copy-done.41, bf16[256,2304]{1,0:T(8,128)(2,1)S(1)} %copy-done.39, bf16[192,1152]{1,0:T(8,128)(2,1)S(1)} %copy-done.45, ...), custom_call_target="tpu_custom_call" | custom-call | flops 22000001024 | tf_op jit(solution)/shard_map/attention_backward/pallas_call | solution.py:38
  124.3 1.6 collective-permute-start.12
  125.9 1.3 far_grads.1
  127.4 12.2 %attention_backward.4 = (bf16[96,1152]{1,0:T(8,128)(2,1)S(1)}, bf16[96,2304]{1,0:T(8,128)(2,1)S(1)}, bf16[96,2304]{1,0:T(8,128)(2,1)S(1)}) custom-call(bf16[192,1152]{1,0:T(8,128)(2,1)S(1)} %get-tuple-element.140.query, bf16[192,2304]{1,0:T(8,128)(2,1)S(1)} %get-tuple-element.99.key, bf16[256,2304]{1,0:T(8,128)(2,1)S(1)} %get-tuple-element.100.value, ...), custom_call_target="tpu_custom_call" | custom-call | flops 11000000512 | tf_op jit(solution)/shard_map/attention_backward/pallas_call | solution.py:38
  139.7 1.3 collective-permute-start.15
  141.2 1.6 collective-permute-start.14
  142.8 12.2 %attention_backward.5 = (bf16[96,1152]{1,0:T(8,128)(2,1)S(1)}, bf16[96,2304]{1,0:T(8,128)(2,1)S(1)}, bf16[96,2304]{1,0:T(8,128)(2,1)S(1)}) custom-call(bf16[192,1152]{1,0:T(8,128)(2,1)S(1)} %get-tuple-element.140.query, bf16[192,2304]{1,0:T(8,128)(2,1)S(1)} %get-tuple-element.99.key, bf16[256,2304]{1,0:T(8,128)(2,1)S(1)} %get-tuple-element.100.value, ...), custom_call_target="tpu_custom_call" | custom-call | flops 11000000512 | tf_op jit(solution)/shard_map/attention_backward/pallas_call | solution.py:38
  155.3 4.5 %post_step.1 = (f32[1152,384]{1,0:T(8,128)S(1)}, bf16[1152,384]{1,0:T(8,128)(2,1)S(1)}, bf16[288,384]{1,0:T(8,128)(2,1)S(1)}, bf16[288,384]{1,0:T(8,128)(2,1)S(1)}, f32[16,384]{1,0:T(8,128)S(1)}) custom-call(bf16[96,1152]{1,0:T(8,128)(2,1)S(1)} %get-tuple-element.135.refs_0_, bf16[96,1152]{1,0:T(8,128)(2,1)S(1)} %get-tuple-element.141.refs_1_, ...), custom_call_target="tpu_custom_call" | custom-call | flops 8000000000 | tf_op jit(solution)/shard_map/post_step/pallas_call | solution.py:38
  160.3 2.6 %collective-permute-start.27 = (bf16[544,384]{1,0:T(8,128)(2,1)S(1)}, bf16[544,384]{1,0:T(8,128)(2,1)S(1)}, u32[]{:S(2)}, u32[]{:S(2)}) collective-permute-start(bf16[544,384]{1,0:T(8,128)(2,1)S(1)} %fold.20.left), channel_id=1, source_target_pairs={{0,16},{4,20},{8,24},{12,28},{16,0},{20,4},{24,8},{28,12},{1,17},{... | collective-permute-start | bytes 1253384 | tf_op jit(solution)/shard_map/ppermute | solution.py:693
  164.1 0.8 collective-permute-start.18
  164.9 1.4 finish.1
  166.3 1.6 collective-permute-done.18.right
  167.9 1.1 collective-permute-start.20
  169.0 2.2 %collective-permute-done.21.right = bf16[288,384]{1,0:T(8,128)(2,1)S(1)} collective-permute-done((bf16[288,384]{1,0:T(8,128)(2,1)S(1)}, bf16[288,384]{1,0:T(8,128)(2,1)S(1)}, u32[]{:S(2)}, u32[]{:S(2)}) %collective-permute-start.21) | collective-permute-done | bytes 221216 | tf_op jit(solution)/shard_map/ppermute | solution.py:693
  171.8 10.0 %collective-permute-done.27.right = bf16[544,384]{1,0:T(8,128)(2,1)S(1)} collective-permute-done((bf16[544,384]{1,0:T(8,128)(2,1)S(1)}, bf16[544,384]{1,0:T(8,128)(2,1)S(1)}, u32[]{:S(2)}, u32[]{:S(2)}) %collective-permute-start.27) | collective-permute-done | bytes 417824 | tf_op jit(solution)/shard_map/ppermute | solution.py:693
  182.5 0.8 collective-permute-start.26
  183.3 2.0 collective-permute-start.22
  185.3 4.8 %collective-permute-done.23.right = bf16[288,384]{1,0:T(8,128)(2,1)S(1)} collective-permute-done((bf16[288,384]{1,0:T(8,128)(2,1)S(1)}, bf16[288,384]{1,0:T(8,128)(2,1)S(1)}, u32[]{:S(2)}, u32[]{:S(2)}) %collective-permute-start.23) | collective-permute-done | bytes 221216 | tf_op jit(solution)/shard_map/ppermute | solution.py:693
  190.1 1.3 collective-permute-start.25
  191.4 1.7 collective-permute-start.24
  194.1 1.5 bitcast_convert_fusion
  195.7 0.8 multiply_add_fusion.8
  196.6 1.9 multiply_add_fusion.2
  198.5 1.3 maximum_select_fusion
  200.6 1.4 multiply_add_fusion
  203.2 1.2 multiply_add_fusion.6
  (203 shorter events, 13.5 us)
Async XLA Ops:
  2.9 13.4 %collective-permute-start = (bf16[576,384]{1,0:T(8,128)(2,1)}, bf16[576,384]{1,0:T(8,128)(2,1)}, u32[]{:S(2)}, u32[]{:S(2)}) collective-permute-start(bf16[576,384]{1,0:T(8,128)(2,1)} %take.1), channel_id=1, source_target_pairs={{0,2},{2,0},{1,3},{3,1},{4,6},{6,4},{5,7},{7,5},{8,10},{10,8},{9,1... | collective-permute-start | bytes 1327112 | tf_op jit(solution)/shard_map/ppermute | solution.py:689
  5.8 14.3 %collective-permute-start.1 = (bf16[2,576,384]{2,1,0:T(8,128)(2,1)}, bf16[2,576,384]{2,1,0:T(8,128)(2,1)}, u32[]{:S(2)}, u32[]{:S(2)}) collective-permute-start(bf16[2,576,384]{2,1,0:T(8,128)(2,1)} %frames.1), channel_id=1, source_target_pairs={{0,1},{1,0},{2,3},{3,2},{4,5},{5,4},{6,7},{7,6},{8,9},{9,8},{10,11... | collective-permute-start | bytes 2654216 | tf_op jit(solution)/shard_map/ppermute | solution.py:685
  6.5 14.4 %copy-start.13 = (f32[9,384]{1,0:T(8,128)S(1)}, f32[9,384]{1,0:T(8,128)}, u32[]{:S(2)}) copy-start(f32[9,384]{1,0:T(8,128)} %vectors.5) | copy-start | bytes 41476
  8.2 18.4 %copy-start.19 = (bf16[576,384]{1,0:T(8,128)(2,1)}, bf16[576,384]{1,0:T(8,128)(2,1)S(1)}, u32[]{:S(2)}) copy-start(bf16[576,384]{1,0:T(8,128)(2,1)S(1)} %get-tuple-element.113) | copy-start | bytes 1327108
  16.3 3.8 %collective-permute-start.2 = (bf16[576,384]{1,0:T(8,128)(2,1)}, bf16[576,384]{1,0:T(8,128)(2,1)S(1)}, u32[]{:S(2)}, u32[]{:S(2)}) collective-permute-start(bf16[576,384]{1,0:T(8,128)(2,1)} %collective-permute-done.got), channel_id=1, source_target_pairs={{0,1},{1,0},{2,3},{3,2},{4,5},{5,4},{6,7},{7,6},{8,9},{9,8},{10,11... | collective-permute-start | bytes 1327112 | tf_op jit(solution)/shard_map/ppermute | solution.py:685
  16.3 3.2 %collective-permute-start.3 = (bf16[288,384]{1,0:T(8,128)(2,1)S(1)}, bf16[288,384]{1,0:T(8,128)(2,1)S(1)}, u32[]{:S(2)}, u32[]{:S(2)}) collective-permute-start(bf16[288,384]{1,0:T(8,128)(2,1)S(1)} %get-tuple-element.104.left.refs_13_), channel_id=1, source_target_pairs={{0,1},{1,0},{2,3},{3,2},{4,5},{5,4},{6,7},{7,6},{8,9},{9,8},{10,11... | collective-permute-start | bytes 663560 | tf_op jit(solution)/shard_map/ppermute | solution.py:685
  16.8 46.2 %collective-permute-start.7 = (bf16[880,384]{1,0:T(8,128)(2,1)}, bf16[880,384]{1,0:T(8,128)(2,1)}, u32[]{:S(2)}, u32[]{:S(2)}) collective-permute-start(bf16[880,384]{1,0:T(8,128)(2,1)} %get-tuple-element.115.refs_0_), channel_id=1, source_target_pairs={{0,1},{1,0},{2,3},{3,2},{4,5},{5,4},{6,7},{7,6},{8,9},{9,8},{10,11... | collective-permute-start | bytes 2027528 | tf_op jit(solution)/shard_map/ppermute | solution.py:685
  17.7 9.6 %collective-permute-start.4 = (bf16[288,384]{1,0:T(8,128)(2,1)S(1)}, bf16[288,384]{1,0:T(8,128)(2,1)S(1)}, u32[]{:S(2)}, u32[]{:S(2)}) collective-permute-start(bf16[288,384]{1,0:T(8,128)(2,1)S(1)} %get-tuple-element.104.left.refs_13_), channel_id=1, source_target_pairs={{0,2},{2,0},{1,3},{3,1},{4,6},{6,4},{5,7},{7,5},{8,10},{10,8},{9,1... | collective-permute-start | bytes 663560 | tf_op jit(solution)/shard_map/ppermute | solution.py:689
  27.3 16.9 %copy-start.36 = (bf16[2304,384]{1,0:T(8,128)(2,1)}, bf16[2304,384]{1,0:T(8,128)(2,1)S(1)}, u32[]{:S(2)}) copy-start(bf16[2304,384]{1,0:T(8,128)(2,1)S(1)} %get-tuple-element.147.first.refs_9_) | copy-start | bytes 5308420
  27.3 35.8 %copy-start.32 = (bf16[2304,384]{1,0:T(8,128)(2,1)}, bf16[2304,384]{1,0:T(8,128)(2,1)S(1)}, u32[]{:S(2)}) copy-start(bf16[2304,384]{1,0:T(8,128)(2,1)S(1)} %get-tuple-element.111.frames.refs_10_) | copy-start | bytes 5308420
  27.3 16.9 %copy-start.28 = (bf16[288,384]{1,0:T(8,128)(2,1)}, bf16[288,384]{1,0:T(8,128)(2,1)S(1)}, u32[]{:S(2)}) copy-start(bf16[288,384]{1,0:T(8,128)(2,1)S(1)} %collective-permute-done.4.refs_0_.refs_15_) | copy-start | bytes 663556
  27.3 16.9 %collective-permute-start.5 = (bf16[288,384]{1,0:T(8,128)(2,1)S(1)}, bf16[288,384]{1,0:T(8,128)(2,1)S(1)}, u32[]{:S(2)}, u32[]{:S(2)}) collective-permute-start(bf16[288,384]{1,0:T(8,128)(2,1)S(1)} %collective-permute-done.4.refs_0_.refs_15_), channel_id=1, source_target_pairs={{0,1},{1,0},{2,3},{3,2},{4,5},{5,4},{6,7},{7,6},{8,9},{9,8},{10,11... | collective-permute-start | bytes 663560 | tf_op jit(solution)/shard_map/ppermute | solution.py:685
  27.6 19.5 %collective-permute-start.8 = (bf16[880,384]{1,0:T(8,128)(2,1)}, bf16[880,384]{1,0:T(8,128)(2,1)S(1)}, u32[]{:S(2)}, u32[]{:S(2)}) collective-permute-start(bf16[880,384]{1,0:T(8,128)(2,1)} %get-tuple-element.115.refs_0_), channel_id=1, source_target_pairs={{0,2},{2,0},{1,3},{3,1},{4,6},{6,4},{5,7},{7,5},{8,10},{10,8},{9,1... | collective-permute-start | bytes 2027528 | tf_op jit(solution)/shard_map/ppermute | solution.py:689
  45.7 17.2 %copy-start.38 = (bf16[256,2304]{1,0:T(8,128)(2,1)}, bf16[256,2304]{1,0:T(8,128)(2,1)S(1)}, u32[]{:S(2)}) copy-start(bf16[256,2304]{1,0:T(8,128)(2,1)S(1)} %get-tuple-element.108.value) | copy-start | bytes 3538948
  45.7 17.2 %copy-start.40 = (bf16[192,2304]{1,0:T(8,128)(2,1)}, bf16[192,2304]{1,0:T(8,128)(2,1)S(1)}, u32[]{:S(2)}) copy-start(bf16[192,2304]{1,0:T(8,128)(2,1)S(1)} %get-tuple-element.107.key) | copy-start | bytes 2654212
  45.7 17.2 %copy-start.42 = (bf16[192,1152]{1,0:T(8,128)(2,1)}, bf16[192,1152]{1,0:T(8,128)(2,1)S(1)}, u32[]{:S(2)}) copy-start(bf16[192,1152]{1,0:T(8,128)(2,1)S(1)} %get-tuple-element.121.query) | copy-start | bytes 1327108
  45.7 17.3 %collective-permute-start.6 = (bf16[576,384]{1,0:T(8,128)(2,1)S(1)}, bf16[576,384]{1,0:T(8,128)(2,1)S(1)}, u32[]{:S(2)}, u32[]{:S(2)}) collective-permute-start(bf16[576,384]{1,0:T(8,128)(2,1)S(1)} %copy-done.20), channel_id=1, source_target_pairs={{0,2},{2,0},{1,3},{3,1},{4,6},{6,4},{5,7},{7,5},{8,10},{10,8},{9,1... | collective-permute-start | bytes 1327112 | tf_op jit(solution)/shard_map/ppermute | solution.py:689
  47.0 16.0 %collective-permute-start.9 = (bf16[880,384]{1,0:T(8,128)(2,1)S(1)}, bf16[880,384]{1,0:T(8,128)(2,1)S(1)}, u32[]{:S(2)}, u32[]{:S(2)}) collective-permute-start(bf16[880,384]{1,0:T(8,128)(2,1)S(1)} %collective-permute-done.8.refs_2_), channel_id=1, source_target_pairs={{0,1},{1,0},{2,3},{3,2},{4,5},{5,4},{6,7},{7,6},{8,9},{9,8},{10,11... | collective-permute-start | bytes 2027528 | tf_op jit(solution)/shard_map/ppermute | solution.py:685
  47.0 16.0 %copy-start.6 = (f32[384,384]{1,0:T(8,128)S(1)}, f32[384,384]{1,0:T(8,128)}, u32[]{:S(2)}) copy-start(f32[384,384]{1,0:T(8,128)} %head.1) | copy-start | bytes 1769476
  47.0 16.0 %copy-start.14 = (f32[9,384]{1,0:T(8,128)S(1)}, f32[9,384]{1,0:T(8,128)}, u32[]{:S(2)}) copy-start(f32[9,384]{1,0:T(8,128)} %vectors.5) | copy-start | bytes 41476
  47.1 16.0 %copy-start.18 = (bf16[2,576,384]{2,1,0:T(8,128)(2,1)S(1)}, bf16[2,576,384]{2,1,0:T(8,128)(2,1)}, u32[]{:S(2)}) copy-start(bf16[2,576,384]{2,1,0:T(8,128)(2,1)} %targets.3) | copy-start | bytes 2654212
  62.9 26.3 %copy-start.44 = (bf16[192,1152]{1,0:T(8,128)(2,1)}, bf16[192,1152]{1,0:T(8,128)(2,1)S(1)}, u32[]{:S(2)}) copy-start(bf16[192,1152]{1,0:T(8,128)(2,1)S(1)} %get-tuple-element.110.attended_far.mixed) | copy-start | bytes 1327108
  63.0 26.3 %copy-start.48 = (f32[4,1152]{1,0:T(4,128)}, f32[4,1152]{1,0:T(4,128)S(1)}, u32[]{:S(2)}) copy-start(f32[4,1152]{1,0:T(4,128)S(1)} %get-tuple-element.123.totals) | copy-start | bytes 55300
  93.0 3.8 %collective-permute-start.10 = (bf16[1952,384]{1,0:T(8,128)(2,1)}, bf16[1952,384]{1,0:T(8,128)(2,1)}, u32[]{:S(2)}, u32[]{:S(2)}) collective-permute-start(bf16[1952,384]{1,0:T(8,128)(2,1)} %get-tuple-element.118), channel_id=1, source_target_pairs={{0,1},{1,0},{2,3},{3,2},{4,5},{5,4},{6,7},{7,6},{8,9},{9,8},{10,11... | collective-permute-start | bytes 4497416 | tf_op jit(solution)/shard_map/ppermute | solution.py:685
  100.1 24.0 %collective-permute-start.11 = (bf16[1088,384]{1,0:T(8,128)(2,1)S(1)}, bf16[1088,384]{1,0:T(8,128)(2,1)S(1)}, u32[]{:S(2)}, u32[]{:S(2)}) collective-permute-start(bf16[1088,384]{1,0:T(8,128)(2,1)S(1)} %get-tuple-element.120), channel_id=1, source_target_pairs={{0,2},{2,0},{1,3},{3,1},{4,6},{6,4},{5,7},{7,5},{8,10},{10,8},{9,1... | collective-permute-start | bytes 2506760 | tf_op jit(solution)/shard_map/ppermute | solution.py:689
  102.0 24.0 %copy-start.37 = (bf16[2304,384]{1,0:T(8,128)(2,1)S(1)}, bf16[2304,384]{1,0:T(8,128)(2,1)}, u32[]{:S(2)}) copy-start(bf16[2304,384]{1,0:T(8,128)(2,1)} %copy-done.36) | copy-start | bytes 5308420
  124.3 16.6 %collective-permute-start.12 = (bf16[544,384]{1,0:T(8,128)(2,1)S(1)}, bf16[544,384]{1,0:T(8,128)(2,1)S(1)}, u32[]{:S(2)}, u32[]{:S(2)}) collective-permute-start(bf16[544,384]{1,0:T(8,128)(2,1)S(1)} %get-tuple-element.127), channel_id=1, source_target_pairs={{0,4},{4,0},{8,12},{12,8},{16,20},{20,16},{24,28},{28,24},{1,5},{5... | collective-permute-start | bytes 1253384 | tf_op jit(solution)/shard_map/ppermute | solution.py:693
  127.3 12.3 %collective-permute-start.13 = (bf16[288,384]{1,0:T(8,128)(2,1)S(1)}, bf16[288,384]{1,0:T(8,128)(2,1)S(1)}, u32[]{:S(2)}, u32[]{:S(2)}) collective-permute-start(bf16[288,384]{1,0:T(8,128)(2,1)S(1)} %get-tuple-element.131), channel_id=1, source_target_pairs={{0,1},{1,0},{2,3},{3,2},{4,5},{5,4},{6,7},{7,6},{8,9},{9,8},{10,11... | collective-permute-start | bytes 663560 | tf_op jit(solution)/shard_map/ppermute | solution.py:685
  139.7 15.5 %collective-permute-start.15 = (bf16[288,384]{1,0:T(8,128)(2,1)S(1)}, bf16[288,384]{1,0:T(8,128)(2,1)S(1)}, u32[]{:S(2)}, u32[]{:S(2)}) collective-permute-start(bf16[288,384]{1,0:T(8,128)(2,1)S(1)} %fold.19), channel_id=1, source_target_pairs={{0,2},{2,0},{1,3},{3,1},{4,6},{6,4},{5,7},{7,5},{8,10},{10,8},{9,1... | collective-permute-start | bytes 663560 | tf_op jit(solution)/shard_map/ppermute | solution.py:689
  141.1 14.1 %copy-start.15 = (f32[9,384]{1,0:T(8,128)S(1)}, f32[9,384]{1,0:T(8,128)}, u32[]{:S(2)}) copy-start(f32[9,384]{1,0:T(8,128)} %vectors.5) | copy-start | bytes 41476
  141.1 14.1 %copy-start.24 = (bf16[288,384]{1,0:T(8,128)(2,1)S(1)}, bf16[288,384]{1,0:T(8,128)(2,1)}, u32[]{:S(2)}) copy-start(bf16[288,384]{1,0:T(8,128)(2,1)} %copy-done.23) | copy-start | bytes 663556
  141.1 14.1 %copy-start.27 = (bf16[288,384]{1,0:T(8,128)(2,1)S(1)}, bf16[288,384]{1,0:T(8,128)(2,1)}, u32[]{:S(2)}) copy-start(bf16[288,384]{1,0:T(8,128)(2,1)} %copy-done.25) | copy-start | bytes 663556
  141.1 14.1 %copy-start.29 = (bf16[288,384]{1,0:T(8,128)(2,1)S(1)}, bf16[288,384]{1,0:T(8,128)(2,1)}, u32[]{:S(2)}) copy-start(bf16[288,384]{1,0:T(8,128)(2,1)} %copy-done.28) | copy-start | bytes 663556
  141.2 13.9 %collective-permute-start.14 = (bf16[544,384]{1,0:T(8,128)(2,1)S(1)}, bf16[544,384]{1,0:T(8,128)(2,1)S(1)}, u32[]{:S(2)}, u32[]{:S(2)}) collective-permute-start(bf16[544,384]{1,0:T(8,128)(2,1)S(1)} %fold.18.left), channel_id=1, source_target_pairs={{0,8},{4,12},{8,0},{12,4},{16,24},{20,28},{24,16},{28,20},{1,9},{5... | collective-permute-start | bytes 1253384 | tf_op jit(solution)/shard_map/ppermute | solution.py:693
  159.7 5.2 %collective-permute-start.19 = (bf16[1152,384]{1,0:T(8,128)(2,1)S(1)}, bf16[1152,384]{1,0:T(8,128)(2,1)S(1)}, u32[]{:S(2)}, u32[]{:S(2)}) collective-permute-start(bf16[1152,384]{1,0:T(8,128)(2,1)S(1)} %get-tuple-element.154), channel_id=1, source_target_pairs={{0,1},{1,0},{2,3},{3,2},{4,5},{5,4},{6,7},{7,6},{8,9},{9,8},{10,11... | collective-permute-start | bytes 2654216 | tf_op jit(solution)/shard_map/ppermute | solution.py:685
  159.8 3.1 %collective-permute-start.17 = (bf16[288,384]{1,0:T(8,128)(2,1)S(1)}, bf16[288,384]{1,0:T(8,128)(2,1)S(1)}, u32[]{:S(2)}, u32[]{:S(2)}) collective-permute-start(bf16[288,384]{1,0:T(8,128)(2,1)S(1)} %get-tuple-element.151), channel_id=1, source_target_pairs={{0,1},{1,0},{2,3},{3,2},{4,5},{5,4},{6,7},{7,6},{8,9},{9,8},{10,11... | collective-permute-start | bytes 663560 | tf_op jit(solution)/shard_map/ppermute | solution.py:685
  160.3 21.5 %collective-permute-start.27 = (bf16[544,384]{1,0:T(8,128)(2,1)S(1)}, bf16[544,384]{1,0:T(8,128)(2,1)S(1)}, u32[]{:S(2)}, u32[]{:S(2)}) collective-permute-start(bf16[544,384]{1,0:T(8,128)(2,1)S(1)} %fold.20.left), channel_id=1, source_target_pairs={{0,16},{4,20},{8,24},{12,28},{16,0},{20,4},{24,8},{28,12},{1,17},{... | collective-permute-start | bytes 1253384 | tf_op jit(solution)/shard_map/ppermute | solution.py:693
  162.9 1.2 collective-permute-start.16
  163.0 8.2 %collective-permute-start.21 = (bf16[288,384]{1,0:T(8,128)(2,1)S(1)}, bf16[288,384]{1,0:T(8,128)(2,1)S(1)}, u32[]{:S(2)}, u32[]{:S(2)}) collective-permute-start(bf16[288,384]{1,0:T(8,128)(2,1)S(1)} %fold.22.left), channel_id=1, source_target_pairs={{0,4},{4,0},{8,12},{12,8},{16,20},{20,16},{24,28},{28,24},{1,5},{5... | collective-permute-start | bytes 663560 | tf_op jit(solution)/shard_map/ppermute | solution.py:693
  164.1 3.8 %collective-permute-start.18 = (f32[16,384]{1,0:T(8,128)S(1)}, f32[16,384]{1,0:T(8,128)S(1)}, u32[]{:S(2)}, u32[]{:S(2)}) collective-permute-start(f32[16,384]{1,0:T(8,128)S(1)} %fold.23.left), channel_id=1, source_target_pairs={{0,2},{2,0},{1,3},{3,1},{4,6},{6,4},{5,7},{7,5},{8,10},{10,8},{9,1... | collective-permute-start | bytes 73736 | tf_op jit(solution)/shard_map/ppermute | solution.py:689
  167.9 3.8 %collective-permute-start.20 = (f32[16,384]{1,0:T(8,128)S(1)}, f32[16,384]{1,0:T(8,128)S(1)}, u32[]{:S(2)}, u32[]{:S(2)}) collective-permute-start(f32[16,384]{1,0:T(8,128)S(1)} %fold.24.left), channel_id=1, source_target_pairs={{0,4},{4,0},{8,12},{12,8},{16,20},{20,16},{24,28},{28,24},{1,5},{5... | collective-permute-start | bytes 73736 | tf_op jit(solution)/shard_map/ppermute | solution.py:693
  181.9 11.4 %collective-permute-start.28 = (bf16[544,384]{1,0:T(8,128)(2,1)S(1)}, bf16[544,384]{1,0:T(8,128)(2,1)S(1)}, u32[]{:S(2)}, u32[]{:S(2)}) collective-permute-start(bf16[544,384]{1,0:T(8,128)(2,1)S(1)} %fold.29.kept), channel_id=1, source_target_pairs={{0,4},{4,0},{8,12},{12,8},{16,20},{20,16},{24,28},{28,24},{1,5},{5... | collective-permute-start | bytes 1253384 | tf_op jit(solution)/shard_map/ppermute | solution.py:693
  182.5 11.7 %collective-permute-start.26 = (bf16[576,384]{1,0:T(8,128)(2,1)S(1)}, bf16[576,384]{1,0:T(8,128)(2,1)}, u32[]{:S(2)}, u32[]{:S(2)}) collective-permute-start(bf16[576,384]{1,0:T(8,128)(2,1)S(1)} %get-tuple-element.163), channel_id=1, source_target_pairs={{0,2},{2,0},{1,3},{3,1},{4,6},{6,4},{5,7},{7,5},{8,10},{10,8},{9,1... | collective-permute-start | bytes 1327112 | tf_op jit(solution)/shard_map/ppermute | solution.py:689
  183.2 6.8 %collective-permute-start.23 = (bf16[288,384]{1,0:T(8,128)(2,1)S(1)}, bf16[288,384]{1,0:T(8,128)(2,1)S(1)}, u32[]{:S(2)}, u32[]{:S(2)}) collective-permute-start(bf16[288,384]{1,0:T(8,128)(2,1)S(1)} %fold.25.left), channel_id=1, source_target_pairs={{0,8},{4,12},{8,0},{12,4},{16,24},{20,28},{24,16},{28,20},{1,9},{5... | collective-permute-start | bytes 663560 | tf_op jit(solution)/shard_map/ppermute | solution.py:693
  183.3 8.2 %collective-permute-start.22 = (f32[16,384]{1,0:T(8,128)S(1)}, f32[16,384]{1,0:T(8,128)S(1)}, u32[]{:S(2)}, u32[]{:S(2)}) collective-permute-start(f32[16,384]{1,0:T(8,128)S(1)} %fold.26.left), channel_id=1, source_target_pairs={{0,8},{4,12},{8,0},{12,4},{16,24},{20,28},{24,16},{28,20},{1,9},{5... | collective-permute-start | bytes 73736 | tf_op jit(solution)/shard_map/ppermute | solution.py:693
  190.1 11.8 %collective-permute-start.25 = (bf16[288,384]{1,0:T(8,128)(2,1)S(1)}, bf16[288,384]{1,0:T(8,128)(2,1)S(1)}, u32[]{:S(2)}, u32[]{:S(2)}) collective-permute-start(bf16[288,384]{1,0:T(8,128)(2,1)S(1)} %fold.27.left), channel_id=1, source_target_pairs={{0,16},{4,20},{8,24},{12,28},{16,0},{20,4},{24,8},{28,12},{1,17},{... | collective-permute-start | bytes 663560 | tf_op jit(solution)/shard_map/ppermute | solution.py:693
  191.4 10.9 %collective-permute-start.24 = (f32[16,384]{1,0:T(8,128)S(1)}, f32[16,384]{1,0:T(8,128)S(1)}, u32[]{:S(2)}, u32[]{:S(2)}) collective-permute-start(f32[16,384]{1,0:T(8,128)S(1)} %fold.28.left), channel_id=1, source_target_pairs={{0,16},{4,20},{8,24},{12,28},{16,0},{20,4},{24,8},{28,12},{1,17},{... | collective-permute-start | bytes 73736 | tf_op jit(solution)/shard_map/ppermute | solution.py:693
  195.6 4.2 %collective-permute-start.29 = (bf16[192,384]{1,0:T(8,128)(2,1)S(1)}, bf16[192,384]{1,0:T(8,128)(2,1)S(1)}, u32[]{:S(2)}, u32[]{:S(2)}) collective-permute-start(bf16[192,384]{1,0:T(8,128)(2,1)S(1)} %slice.47), channel_id=1, source_target_pairs={{0,1},{1,0},{2,3},{3,2},{4,5},{5,4},{6,7},{7,6},{8,9},{9,8},{10,11... | collective-permute-start | bytes 442376 | tf_op jit(solution)/shard_map/ppermute | solution.py:685
  (51 other events, 170.6 us)
where the time goes:
time: 206 us
  Pallas kernels  123 us (60%)
  waiting for transfers between devices  32 us (16%)
  starting transfers between devices  25.7 us (12%)
  local copies, waits for them, and re-layouts  12.7 us (6%)
  other arithmetic  10.2 us (5%)
    pallas_call x30, Pallas kernels, kernel_call(): pl.pallas_call(body, out_shape=outs, in_specs=in_specs or [VMEM] * len(in...  123 us
    ppermute x10, waiting for transfers between devices, swap_dp(): return lax.ppermute(values, 'dp', [(i, i ^ step) for i in range(size)])  17.9 us
    ppermute x10, starting transfers between devices, swap_dp(): return lax.ppermute(values, 'dp', [(i, i ^ step) for i in range(size)])  13.1 us
    unnamed x138, local copies, waits for them, and re-layouts  11.4 us
    ppermute x8, starting transfers between devices, swap_chip(): return lax.ppermute(values, 'tp', CHIP_PAIRS)  10.5 us
    ppermute x8, waiting for transfers between devices, swap_chip(): return lax.ppermute(values, 'tp', CHIP_PAIRS)  10.3 us
    add x6, other arithmetic, update(): average_new = AVERAGE_RATE * average + (1.0 - AVERAGE_RATE) * weight_new  6.51 us
  transfers between devices with their start and end apart: 30, of which 11 were waited for; matrix products, arithmetic and copies ran while one was open for 4% of the time, Pallas kernels for 43%

commit v1 on v0

--- a/solution.py
+++ b/solution.py
@@ -797,10 +797,12 @@
     near_one = backward(0, 0, here // 2, sent, far_sent)
     (far_kept,) = fold(far_kept, tie(got_far, near_one[0]), [[(0, rows)]])
     got_far = swap_chip(far_kept)
-    (kept,) = fold(kept, tie(got_y, near_one[0]), [[(0, full // 2)]])
-    got_z = swap_dp(kept, 2, size)
-    near_two = backward(0, here // 2, here // 2, kept, far_kept)
-    (kept,) = fold(kept, tie(got_z, near_two[0]), [[(0, full // 2)]])
+    kept, sent = fold(
+        kept, tie(got_y, near_one[0]), [[(0, full // 2, bits[1])], [(0, full // 2, others[1])]], spot
+    )
+    got_z = swap_dp(sent, 2, size)
+    near_two = backward(0, here // 2, here // 2, sent, far_kept)
+    (kept,) = fold(kept, tie(got_z, near_two[0]), [[(0, full // 4)]])
     got_step = swap_dp(kept, steps[2], size)
     mine, other, near_kept, near_sent, small = post_step(
         [near_one, near_two, far_all],
@@ -819,8 +821,8 @@
     (small,) = fold(small, tie(got_small, attn_kept), [[(0, SMALL)]], dtype=f32)
     got_small = swap_chip(small)
     own_rows, returned = finish(mine, other_rows, every, vectors, tie(grad_middle, attn_kept, small))
-    returned = swap_chip(returned)
     (small,) = fold(small, tie(got_small, own_rows), [[(0, SMALL)]], dtype=f32)
+    returned = swap_chip(tie(returned, small))
     def settle(kept, got_kept, returned):
         kept = join(kept, got_kept, bits[0], spot)
         returned = returned.astype(f32)
@@ -848,18 +850,22 @@
         got_small = swap_dp(small, step, size)
         if step == steps[-1]:
             last = settle(kept, got_kept, returned)
-            got_attn = tie(got_attn, *last)
+            got_attn = tie(got_attn, last[0])
         (attn_kept,) = fold(
             attn_kept, tie(got_attn, small), [[(0, rows)]], dtype=f32 if step == steps[-1] else bf16
         )
         if step < steps[-1]:
             got_attn = swap_dp(attn_kept, 2 * step, size)
+        if step == 2:
+            kept = join(kept, tie(got_kept, attn_kept), bits[1], spot)
+            got_kept = swap_dp(kept, 1, size)
+            got_small = tie(got_small, kept)
         (small,) = fold(small, tie(got_small, attn_kept), [[(0, SMALL)]], dtype=f32)
         if step == 1:
             for high in steps[2:]:
                 got_step = tie(got_step, small) if high == steps[2] else swap_dp(kept, high, size)
-                (kept,) = fold(kept, got_step, [[(0, full // 2)]])
-            got_kept = swap_dp(kept, 1, size)
+                (kept,) = fold(kept, got_step, [[(0, full // 4)]])
+            got_kept = swap_dp(kept, 2, size)
         elif step == 2:
             returned = tie(returned, attn_kept)
     grad_frames, *sets = last

time: 206 us -> 202 us (0.981)
  waiting for transfers between devices: 32 us -> 28.6 us
    ppermute x10 -> x11, waiting for transfers between devices: 17.9 us -> 15 us  [swap_dp(): return lax.ppermute(values, 'dp', [(i, i ^ step) for i in range(size)])]
    ppermute x10 -> x11, starting transfers between devices: 13.1 us -> 13 us  [swap_dp(): return lax.ppermute(values, 'dp', [(i, i ^ step) for i in range(size)])]
    pallas_call x30 -> x31, Pallas kernels: 123 us -> 123 us  [kernel_call(): pl.pallas_call(body, out_shape=outs, in_specs=in_specs or [VMEM] * len(in...]
  transfers between devices with their start and end apart: 30 -> 31, of which waited for: 11 -> 12; matrix products, arithmetic and copies ran while one was open for 4% -> 4% of each run, Pallas kernels for 43% -> 44%
where the time goes in v1:
time: 202 us
  Pallas kernels  123 us (61%)
  waiting for transfers between devices  28.6 us (14%)
  starting transfers between devices  25.5 us (13%)
  local copies, waits for them, and re-layouts  13.8 us (7%)
  other arithmetic  8.78 us (4%)
    pallas_call x31, Pallas kernels, kernel_call(): pl.pallas_call(body, out_shape=outs, in_specs=in_specs or [VMEM] * len(in...  123 us
    ppermute x11, waiting for transfers between devices, swap_dp(): return lax.ppermute(values, 'dp', [(i, i ^ step) for i in range(size)])  15 us
    ppermute x11, starting transfers between devices, swap_dp(): return lax.ppermute(values, 'dp', [(i, i ^ step) for i in range(size)])  13 us
    unnamed x138, local copies, waits for them, and re-layouts  12.4 us
    ppermute x8, starting transfers between devices, swap_chip(): return lax.ppermute(values, 'tp', CHIP_PAIRS)  10.5 us
    ppermute x8, waiting for transfers between devices, swap_chip(): return lax.ppermute(values, 'tp', CHIP_PAIRS)  9.81 us
    add x6, other arithmetic, update(): average_new = AVERAGE_RATE * average + (1.0 - AVERAGE_RATE) * weight_new  6.53 us
  transfers between devices with their start and end apart: 31, of which 12 were waited for; matrix products, arithmetic and copies ran while one was open for 4% of the time, Pallas kernels for 44%

profile of v1, /device:TPU:0, one launch (start us, length us, event | category | flops | bytes accessed | tf_op | source)
XLA Modules:
  0.0 201.7 jit_solution(2825699149512667163)
XLA Ops:
  0.8 2.1 %take.1 = bf16[576,384]{1,0:T(8,128)(2,1)} custom-call(s32[1]{0:T(128)} %bitcast.1.place, bf16[2,576,384]{2,1,0:T(8,128)(2,1)} %frames.1), custom_call_target="tpu_custom_call" | custom-call | flops 1000000000 | tf_op jit(solution)/shard_map/take/pallas_call | solution.py:38
  2.9 2.9 %collective-permute-start = (bf16[576,384]{1,0:T(8,128)(2,1)}, bf16[576,384]{1,0:T(8,128)(2,1)}, u32[]{:S(2)}, u32[]{:S(2)}) collective-permute-start(bf16[576,384]{1,0:T(8,128)(2,1)} %take.1), channel_id=1, source_target_pairs={{0,2},{2,0},{1,3},{3,1},{4,6},{6,4},{5,7},{7,5},{8,10},{10,8},{9,1... | collective-permute-start | bytes 1327112 | tf_op jit(solution)/shard_map/ppermute | solution.py:689
  6.5 1.6 pack.1
  8.1 8.1 %collective-permute-done.got = bf16[576,384]{1,0:T(8,128)(2,1)} collective-permute-done((bf16[576,384]{1,0:T(8,128)(2,1)}, bf16[576,384]{1,0:T(8,128)(2,1)}, u32[]{:S(2)}, u32[]{:S(2)}) %collective-permute-start) | collective-permute-done | bytes 442400 | tf_op jit(solution)/shard_map/ppermute | solution.py:689
  17.7 1.7 collective-permute-start.4
  20.9 1.0 copy-done.22
  21.9 0.9 copy-done.26
  22.9 3.7 %project_near.1 = (bf16[192,1152]{1,0:T(8,128)(2,1)S(1)}, bf16[192,2304]{1,0:T(8,128)(2,1)S(1)}, bf16[256,2304]{1,0:T(8,128)(2,1)S(1)}, bf16[2304,384]{1,0:T(8,128)(2,1)S(1)}, bf16[2304,384]{1,0:T(8,128)(2,1)S(1)}) custom-call(s32[1]{0:T(128)} %bitcast.place, bf16[2,576,384]{2,1,0:T(8,128)(2,1)} %frames.1, bf16[576,384]{1,0:T(8,128)(2,1)} %collective-permute-done.got, ...), custom_call_target="tpu_custom_call" | custom-call | flops 4000000000 | tf_op jit(solution)/shard_map/project_near/pallas_call | solution.py:38
  27.6 0.8 collective-permute-start.8
  28.3 15.8 %attention_forward.2 = (bf16[192,1152]{1,0:T(8,128)(2,1)S(1)}, f32[4,1152]{1,0:T(4,128)S(1)}, bf16[8,1152,2304]{2,1,0:T(8,128)(2,1)}) custom-call(bf16[192,1152]{1,0:T(8,128)(2,1)S(1)} %get-tuple-element.146.query, bf16[192,2304]{1,0:T(8,128)(2,1)S(1)} %get-tuple-element.104.key, bf16[256,2304]{1,0:T(8,128)(2,1)S(1)} %get-tuple-element.105.value), custom_call_target="tpu_custom_call" | custom-call | flops 16000000000 | tf_op jit(solution)/shard_map/attention_forward/pallas_call | solution.py:38
  44.2 1.4 project_far.1
  45.7 1.3 collective-permute-start.6
  47.1 15.8 %attention_forward.3 = (bf16[192,1152]{1,0:T(8,128)(2,1)S(1)}, f32[4,1152]{1,0:T(4,128)S(1)}, bf16[8,1152,2304]{2,1,0:T(8,128)(2,1)}) custom-call(bf16[192,1152]{1,0:T(8,128)(2,1)S(1)} %get-tuple-element.126.query, bf16[192,2304]{1,0:T(8,128)(2,1)S(1)} %get-tuple-element.112.key, ...), custom_call_target="tpu_custom_call", output_to_operand_aliasing={{2}: (3, {})} | custom-call | flops 16000000000 | tf_op jit(solution)/shard_map/attention_forward/pallas_call | solution.py:38
  63.0 26.3 %middle_step.1 = (f32[1152,384]{1,0:T(8,128)S(1)}, bf16[192,1152]{1,0:T(8,128)(2,1)S(1)}, bf16[192,1152]{1,0:T(8,128)(2,1)S(1)}, bf16[1952,384]{1,0:T(8,128)(2,1...) custom-call(s32[2]{0:T(128)S(1)} %pad_add_fusion.place, ...), custom_call_target="tpu_custom_call" | custom-call | flops 20000000000 | tf_op jit(solution)/shard_map/middle_step/pallas_call | solution.py:38
  89.3 1.1 copy-done
  90.4 1.2 copy-done.34
  91.6 0.8 copy-done.46
  93.5 3.3 %collective-permute-done.10.right = bf16[1952,384]{1,0:T(8,128)(2,1)} collective-permute-done((bf16[1952,384]{1,0:T(8,128)(2,1)}, bf16[1952,384]{1,0:T(8,128)(2,1)}, u32[]{:S(2)}, u32[]{:S(2)}) %collective-permute-start.10) | collective-permute-done | bytes 1499168 | tf_op jit(solution)/shard_map/ppermute | solution.py:685
  96.8 1.4 copy-done.1
  98.2 1.9 fold.16
  100.1 0.9 collective-permute-start.11
  101.0 1.0 copy-done.47
  102.0 22.1 %attention_backward.3 = (bf16[192,1152]{1,0:T(8,128)(2,1)S(1)}, bf16[192,2304]{1,0:T(8,128)(2,1)S(1)}, bf16[192,2304]{1,0:T(8,128)(2,1)S(1)}) custom-call(bf16[192,1152]{1,0:T(8,128)(2,1)S(1)} %copy-done.43, bf16[192,2304]{1,0:T(8,128)(2,1)S(1)} %copy-done.41, bf16[256,2304]{1,0:T(8,128)(2,1)S(1)} %copy-done.39, bf16[192,1152]{1,0:T(8,128)(2,1)S(1)} %copy-done.45, ...), custom_call_target="tpu_custom_call" | custom-call | flops 22000001024 | tf_op jit(solution)/shard_map/attention_backward/pallas_call | solution.py:38
  124.4 1.6 collective-permute-start.12
  126.0 1.3 far_grads.1
  127.4 12.2 %attention_backward.4 = (bf16[96,1152]{1,0:T(8,128)(2,1)S(1)}, bf16[96,2304]{1,0:T(8,128)(2,1)S(1)}, bf16[96,2304]{1,0:T(8,128)(2,1)S(1)}) custom-call(bf16[192,1152]{1,0:T(8,128)(2,1)S(1)} %get-tuple-element.146.query, bf16[192,2304]{1,0:T(8,128)(2,1)S(1)} %get-tuple-element.104.key, bf16[256,2304]{1,0:T(8,128)(2,1)S(1)} %get-tuple-element.105.value, ...), custom_call_target="tpu_custom_call" | custom-call | flops 11000000512 | tf_op jit(solution)/shard_map/attention_backward/pallas_call | solution.py:38
  139.7 1.3 collective-permute-start.15
  141.2 1.6 collective-permute-start.14
  142.8 12.2 %attention_backward.5 = (bf16[96,1152]{1,0:T(8,128)(2,1)S(1)}, bf16[96,2304]{1,0:T(8,128)(2,1)S(1)}, bf16[96,2304]{1,0:T(8,128)(2,1)S(1)}) custom-call(bf16[192,1152]{1,0:T(8,128)(2,1)S(1)} %get-tuple-element.146.query, bf16[192,2304]{1,0:T(8,128)(2,1)S(1)} %get-tuple-element.104.key, bf16[256,2304]{1,0:T(8,128)(2,1)S(1)} %get-tuple-element.105.value, ...), custom_call_target="tpu_custom_call" | custom-call | flops 11000000512 | tf_op jit(solution)/shard_map/attention_backward/pallas_call | solution.py:38
  155.2 4.5 %post_step.1 = (f32[1152,384]{1,0:T(8,128)S(1)}, bf16[1152,384]{1,0:T(8,128)(2,1)S(1)}, bf16[288,384]{1,0:T(8,128)(2,1)S(1)}, bf16[288,384]{1,0:T(8,128)(2,1)S(1)}, f32[16,384]{1,0:T(8,128)S(1)}) custom-call(bf16[96,1152]{1,0:T(8,128)(2,1)S(1)} %get-tuple-element.140.refs_0_, bf16[96,1152]{1,0:T(8,128)(2,1)S(1)} %get-tuple-element.147.refs_1_, ...), custom_call_target="tpu_custom_call" | custom-call | flops 8000000000 | tf_op jit(solution)/shard_map/post_step/pallas_call | solution.py:38
  160.3 2.6 %collective-permute-start.23 = (bf16[272,384]{1,0:T(8,128)(2,1)S(1)}, bf16[272,384]{1,0:T(8,128)(2,1)S(1)}, u32[]{:S(2)}, u32[]{:S(2)}) collective-permute-start(bf16[272,384]{1,0:T(8,128)(2,1)S(1)} %fold.20.left), channel_id=1, source_target_pairs={{0,16},{4,20},{8,24},{12,28},{16,0},{20,4},{24,8},{28,12},{1,17},{... | collective-permute-start | bytes 626696 | tf_op jit(solution)/shard_map/ppermute | solution.py:693
  164.1 0.8 collective-permute-start.18
  164.9 1.4 finish.1
  166.3 1.6 collective-permute-done.18.right
  167.9 0.8 collective-permute-start.28
  168.7 1.1 collective-permute-start.20
  169.8 1.4 collective-permute-done.21.right
  171.2 0.9 collective-permute-start.25
  173.5 1.5 collective-permute-start.22
  175.0 4.7 %collective-permute-done.25.right = bf16[288,384]{1,0:T(8,128)(2,1)S(1)} collective-permute-done((bf16[288,384]{1,0:T(8,128)(2,1)S(1)}, bf16[288,384]{1,0:T(8,128)(2,1)S(1)}, u32[]{:S(2)}, u32[]{:S(2)}) %collective-permute-start.25) | collective-permute-done | bytes 221216 | tf_op jit(solution)/shard_map/ppermute | solution.py:693
  179.7 1.9 collective-permute-start.27
  181.6 4.5 %collective-permute-done.24.got = bf16[272,384]{1,0:T(8,128)(2,1)S(1)} collective-permute-done((bf16[272,384]{1,0:T(8,128)(2,1)S(1)}, bf16[272,384]{1,0:T(8,128)(2,1)S(1)}, u32[]{:S(2)}, u32[]{:S(2)}) %collective-permute-start.24) | collective-permute-done | bytes 208928 | tf_op jit(solution)/shard_map/ppermute | solution.py:693
  187.0 1.3 maximum_select_fusion
  188.3 2.7 %collective-permute-done.27.right = bf16[288,384]{1,0:T(8,128)(2,1)S(1)} collective-permute-done((bf16[288,384]{1,0:T(8,128)(2,1)S(1)}, bf16[288,384]{1,0:T(8,128)(2,1)S(1)}, u32[]{:S(2)}, u32[]{:S(2)}) %collective-permute-start.27) | collective-permute-done | bytes 221216 | tf_op jit(solution)/shard_map/ppermute | solution.py:693
  193.4 1.2 multiply_add_fusion.6
  197.0 1.9 multiply_add_fusion.1
  198.9 0.8 multiply_add_fusion.8
  200.3 1.4 multiply_add_fusion
  (206 shorter events, 15.6 us)
Async XLA Ops:
  2.9 13.4 %collective-permute-start = (bf16[576,384]{1,0:T(8,128)(2,1)}, bf16[576,384]{1,0:T(8,128)(2,1)}, u32[]{:S(2)}, u32[]{:S(2)}) collective-permute-start(bf16[576,384]{1,0:T(8,128)(2,1)} %take.1), channel_id=1, source_target_pairs={{0,2},{2,0},{1,3},{3,1},{4,6},{6,4},{5,7},{7,5},{8,10},{10,8},{9,1... | collective-permute-start | bytes 1327112 | tf_op jit(solution)/shard_map/ppermute | solution.py:689
  5.8 14.3 %collective-permute-start.1 = (bf16[2,576,384]{2,1,0:T(8,128)(2,1)}, bf16[2,576,384]{2,1,0:T(8,128)(2,1)}, u32[]{:S(2)}, u32[]{:S(2)}) collective-permute-start(bf16[2,576,384]{2,1,0:T(8,128)(2,1)} %frames.1), channel_id=1, source_target_pairs={{0,1},{1,0},{2,3},{3,2},{4,5},{5,4},{6,7},{7,6},{8,9},{9,8},{10,11... | collective-permute-start | bytes 2654216 | tf_op jit(solution)/shard_map/ppermute | solution.py:685
  6.5 14.4 %copy-start.13 = (f32[9,384]{1,0:T(8,128)S(1)}, f32[9,384]{1,0:T(8,128)}, u32[]{:S(2)}) copy-start(f32[9,384]{1,0:T(8,128)} %vectors.5) | copy-start | bytes 41476
  8.1 18.4 %copy-start.19 = (bf16[576,384]{1,0:T(8,128)(2,1)}, bf16[576,384]{1,0:T(8,128)(2,1)S(1)}, u32[]{:S(2)}) copy-start(bf16[576,384]{1,0:T(8,128)(2,1)S(1)} %get-tuple-element.118) | copy-start | bytes 1327108
  16.3 3.8 %collective-permute-start.2 = (bf16[576,384]{1,0:T(8,128)(2,1)}, bf16[576,384]{1,0:T(8,128)(2,1)S(1)}, u32[]{:S(2)}, u32[]{:S(2)}) collective-permute-start(bf16[576,384]{1,0:T(8,128)(2,1)} %collective-permute-done.got), channel_id=1, source_target_pairs={{0,1},{1,0},{2,3},{3,2},{4,5},{5,4},{6,7},{7,6},{8,9},{9,8},{10,11... | collective-permute-start | bytes 1327112 | tf_op jit(solution)/shard_map/ppermute | solution.py:685
  16.3 3.2 %collective-permute-start.3 = (bf16[288,384]{1,0:T(8,128)(2,1)S(1)}, bf16[288,384]{1,0:T(8,128)(2,1)S(1)}, u32[]{:S(2)}, u32[]{:S(2)}) collective-permute-start(bf16[288,384]{1,0:T(8,128)(2,1)S(1)} %get-tuple-element.109.left.refs_13_), channel_id=1, source_target_pairs={{0,1},{1,0},{2,3},{3,2},{4,5},{5,4},{6,7},{7,6},{8,9},{9,8},{10,11... | collective-permute-start | bytes 663560 | tf_op jit(solution)/shard_map/ppermute | solution.py:685
  16.8 46.2 %collective-permute-start.7 = (bf16[880,384]{1,0:T(8,128)(2,1)}, bf16[880,384]{1,0:T(8,128)(2,1)}, u32[]{:S(2)}, u32[]{:S(2)}) collective-permute-start(bf16[880,384]{1,0:T(8,128)(2,1)} %get-tuple-element.120.refs_0_), channel_id=1, source_target_pairs={{0,1},{1,0},{2,3},{3,2},{4,5},{5,4},{6,7},{7,6},{8,9},{9,8},{10,11... | collective-permute-start | bytes 2027528 | tf_op jit(solution)/shard_map/ppermute | solution.py:685
  17.7 9.6 %collective-permute-start.4 = (bf16[288,384]{1,0:T(8,128)(2,1)S(1)}, bf16[288,384]{1,0:T(8,128)(2,1)S(1)}, u32[]{:S(2)}, u32[]{:S(2)}) collective-permute-start(bf16[288,384]{1,0:T(8,128)(2,1)S(1)} %get-tuple-element.109.left.refs_13_), channel_id=1, source_target_pairs={{0,2},{2,0},{1,3},{3,1},{4,6},{6,4},{5,7},{7,5},{8,10},{10,8},{9,1... | collective-permute-start | bytes 663560 | tf_op jit(solution)/shard_map/ppermute | solution.py:689
  27.3 16.9 %copy-start.36 = (bf16[2304,384]{1,0:T(8,128)(2,1)}, bf16[2304,384]{1,0:T(8,128)(2,1)S(1)}, u32[]{:S(2)}) copy-start(bf16[2304,384]{1,0:T(8,128)(2,1)S(1)} %get-tuple-element.154.first.refs_9_) | copy-start | bytes 5308420
  27.3 35.8 %copy-start.32 = (bf16[2304,384]{1,0:T(8,128)(2,1)}, bf16[2304,384]{1,0:T(8,128)(2,1)S(1)}, u32[]{:S(2)}) copy-start(bf16[2304,384]{1,0:T(8,128)(2,1)S(1)} %get-tuple-element.116.frames.refs_10_) | copy-start | bytes 5308420
  27.3 16.9 %copy-start.28 = (bf16[288,384]{1,0:T(8,128)(2,1)}, bf16[288,384]{1,0:T(8,128)(2,1)S(1)}, u32[]{:S(2)}) copy-start(bf16[288,384]{1,0:T(8,128)(2,1)S(1)} %collective-permute-done.4.refs_0_.refs_15_) | copy-start | bytes 663556
  27.3 16.9 %collective-permute-start.5 = (bf16[288,384]{1,0:T(8,128)(2,1)S(1)}, bf16[288,384]{1,0:T(8,128)(2,1)S(1)}, u32[]{:S(2)}, u32[]{:S(2)}) collective-permute-start(bf16[288,384]{1,0:T(8,128)(2,1)S(1)} %collective-permute-done.4.refs_0_.refs_15_), channel_id=1, source_target_pairs={{0,1},{1,0},{2,3},{3,2},{4,5},{5,4},{6,7},{7,6},{8,9},{9,8},{10,11... | collective-permute-start | bytes 663560 | tf_op jit(solution)/shard_map/ppermute | solution.py:685
  27.6 19.5 %collective-permute-start.8 = (bf16[880,384]{1,0:T(8,128)(2,1)}, bf16[880,384]{1,0:T(8,128)(2,1)S(1)}, u32[]{:S(2)}, u32[]{:S(2)}) collective-permute-start(bf16[880,384]{1,0:T(8,128)(2,1)} %get-tuple-element.120.refs_0_), channel_id=1, source_target_pairs={{0,2},{2,0},{1,3},{3,1},{4,6},{6,4},{5,7},{7,5},{8,10},{10,8},{9,1... | collective-permute-start | bytes 2027528 | tf_op jit(solution)/shard_map/ppermute | solution.py:689
  45.7 17.2 %copy-start.38 = (bf16[256,2304]{1,0:T(8,128)(2,1)}, bf16[256,2304]{1,0:T(8,128)(2,1)S(1)}, u32[]{:S(2)}) copy-start(bf16[256,2304]{1,0:T(8,128)(2,1)S(1)} %get-tuple-element.113.value) | copy-start | bytes 3538948
  45.7 17.2 %copy-start.40 = (bf16[192,2304]{1,0:T(8,128)(2,1)}, bf16[192,2304]{1,0:T(8,128)(2,1)S(1)}, u32[]{:S(2)}) copy-start(bf16[192,2304]{1,0:T(8,128)(2,1)S(1)} %get-tuple-element.112.key) | copy-start | bytes 2654212
  45.7 17.2 %copy-start.42 = (bf16[192,1152]{1,0:T(8,128)(2,1)}, bf16[192,1152]{1,0:T(8,128)(2,1)S(1)}, u32[]{:S(2)}) copy-start(bf16[192,1152]{1,0:T(8,128)(2,1)S(1)} %get-tuple-element.126.query) | copy-start | bytes 1327108
  45.7 17.3 %collective-permute-start.6 = (bf16[576,384]{1,0:T(8,128)(2,1)S(1)}, bf16[576,384]{1,0:T(8,128)(2,1)S(1)}, u32[]{:S(2)}, u32[]{:S(2)}) collective-permute-start(bf16[576,384]{1,0:T(8,128)(2,1)S(1)} %copy-done.20), channel_id=1, source_target_pairs={{0,2},{2,0},{1,3},{3,1},{4,6},{6,4},{5,7},{7,5},{8,10},{10,8},{9,1... | collective-permute-start | bytes 1327112 | tf_op jit(solution)/shard_map/ppermute | solution.py:689
  47.0 15.9 %collective-permute-start.9 = (bf16[880,384]{1,0:T(8,128)(2,1)S(1)}, bf16[880,384]{1,0:T(8,128)(2,1)S(1)}, u32[]{:S(2)}, u32[]{:S(2)}) collective-permute-start(bf16[880,384]{1,0:T(8,128)(2,1)S(1)} %collective-permute-done.8.refs_2_), channel_id=1, source_target_pairs={{0,1},{1,0},{2,3},{3,2},{4,5},{5,4},{6,7},{7,6},{8,9},{9,8},{10,11... | collective-permute-start | bytes 2027528 | tf_op jit(solution)/shard_map/ppermute | solution.py:685
  47.0 16.0 %copy-start.6 = (f32[384,384]{1,0:T(8,128)S(1)}, f32[384,384]{1,0:T(8,128)}, u32[]{:S(2)}) copy-start(f32[384,384]{1,0:T(8,128)} %head.1) | copy-start | bytes 1769476
  47.1 16.0 %copy-start.14 = (f32[9,384]{1,0:T(8,128)S(1)}, f32[9,384]{1,0:T(8,128)}, u32[]{:S(2)}) copy-start(f32[9,384]{1,0:T(8,128)} %vectors.5) | copy-start | bytes 41476
  47.1 16.0 %copy-start.18 = (bf16[2,576,384]{2,1,0:T(8,128)(2,1)S(1)}, bf16[2,576,384]{2,1,0:T(8,128)(2,1)}, u32[]{:S(2)}) copy-start(bf16[2,576,384]{2,1,0:T(8,128)(2,1)} %targets.3) | copy-start | bytes 2654212
  62.9 26.4 %copy-start.44 = (bf16[192,1152]{1,0:T(8,128)(2,1)}, bf16[192,1152]{1,0:T(8,128)(2,1)S(1)}, u32[]{:S(2)}) copy-start(bf16[192,1152]{1,0:T(8,128)(2,1)S(1)} %get-tuple-element.115.attended_far.mixed) | copy-start | bytes 1327108
  63.0 26.3 %copy-start.48 = (f32[4,1152]{1,0:T(4,128)}, f32[4,1152]{1,0:T(4,128)S(1)}, u32[]{:S(2)}) copy-start(f32[4,1152]{1,0:T(4,128)S(1)} %get-tuple-element.128.totals) | copy-start | bytes 55300
  93.0 3.8 %collective-permute-start.10 = (bf16[1952,384]{1,0:T(8,128)(2,1)}, bf16[1952,384]{1,0:T(8,128)(2,1)}, u32[]{:S(2)}, u32[]{:S(2)}) collective-permute-start(bf16[1952,384]{1,0:T(8,128)(2,1)} %get-tuple-element.123), channel_id=1, source_target_pairs={{0,1},{1,0},{2,3},{3,2},{4,5},{5,4},{6,7},{7,6},{8,9},{9,8},{10,11... | collective-permute-start | bytes 4497416 | tf_op jit(solution)/shard_map/ppermute | solution.py:685
  100.1 24.0 %collective-permute-start.11 = (bf16[1088,384]{1,0:T(8,128)(2,1)S(1)}, bf16[1088,384]{1,0:T(8,128)(2,1)S(1)}, u32[]{:S(2)}, u32[]{:S(2)}) collective-permute-start(bf16[1088,384]{1,0:T(8,128)(2,1)S(1)} %get-tuple-element.125), channel_id=1, source_target_pairs={{0,2},{2,0},{1,3},{3,1},{4,6},{6,4},{5,7},{7,5},{8,10},{10,8},{9,1... | collective-permute-start | bytes 2506760 | tf_op jit(solution)/shard_map/ppermute | solution.py:689
  102.0 24.0 %copy-start.37 = (bf16[2304,384]{1,0:T(8,128)(2,1)S(1)}, bf16[2304,384]{1,0:T(8,128)(2,1)}, u32[]{:S(2)}) copy-start(bf16[2304,384]{1,0:T(8,128)(2,1)} %copy-done.36) | copy-start | bytes 5308420
  124.4 16.6 %collective-permute-start.12 = (bf16[544,384]{1,0:T(8,128)(2,1)S(1)}, bf16[544,384]{1,0:T(8,128)(2,1)S(1)}, u32[]{:S(2)}, u32[]{:S(2)}) collective-permute-start(bf16[544,384]{1,0:T(8,128)(2,1)S(1)} %get-tuple-element.132), channel_id=1, source_target_pairs={{0,4},{4,0},{8,12},{12,8},{16,20},{20,16},{24,28},{28,24},{1,5},{5... | collective-permute-start | bytes 1253384 | tf_op jit(solution)/shard_map/ppermute | solution.py:693
  127.3 12.3 %collective-permute-start.13 = (bf16[288,384]{1,0:T(8,128)(2,1)S(1)}, bf16[288,384]{1,0:T(8,128)(2,1)S(1)}, u32[]{:S(2)}, u32[]{:S(2)}) collective-permute-start(bf16[288,384]{1,0:T(8,128)(2,1)S(1)} %get-tuple-element.136), channel_id=1, source_target_pairs={{0,1},{1,0},{2,3},{3,2},{4,5},{5,4},{6,7},{7,6},{8,9},{9,8},{10,11... | collective-permute-start | bytes 663560 | tf_op jit(solution)/shard_map/ppermute | solution.py:685
  139.7 15.5 %collective-permute-start.15 = (bf16[288,384]{1,0:T(8,128)(2,1)S(1)}, bf16[288,384]{1,0:T(8,128)(2,1)S(1)}, u32[]{:S(2)}, u32[]{:S(2)}) collective-permute-start(bf16[288,384]{1,0:T(8,128)(2,1)S(1)} %fold.19), channel_id=1, source_target_pairs={{0,2},{2,0},{1,3},{3,1},{4,6},{6,4},{5,7},{7,5},{8,10},{10,8},{9,1... | collective-permute-start | bytes 663560 | tf_op jit(solution)/shard_map/ppermute | solution.py:689
  141.1 14.1 %copy-start.15 = (f32[9,384]{1,0:T(8,128)S(1)}, f32[9,384]{1,0:T(8,128)}, u32[]{:S(2)}) copy-start(f32[9,384]{1,0:T(8,128)} %vectors.5) | copy-start | bytes 41476
  141.1 14.1 %copy-start.24 = (bf16[288,384]{1,0:T(8,128)(2,1)S(1)}, bf16[288,384]{1,0:T(8,128)(2,1)}, u32[]{:S(2)}) copy-start(bf16[288,384]{1,0:T(8,128)(2,1)} %copy-done.23) | copy-start | bytes 663556
  141.1 14.0 %copy-start.27 = (bf16[288,384]{1,0:T(8,128)(2,1)S(1)}, bf16[288,384]{1,0:T(8,128)(2,1)}, u32[]{:S(2)}) copy-start(bf16[288,384]{1,0:T(8,128)(2,1)} %copy-done.25) | copy-start | bytes 663556
  141.2 13.9 %collective-permute-start.14 = (bf16[272,384]{1,0:T(8,128)(2,1)S(1)}, bf16[272,384]{1,0:T(8,128)(2,1)S(1)}, u32[]{:S(2)}, u32[]{:S(2)}) collective-permute-start(bf16[272,384]{1,0:T(8,128)(2,1)S(1)} %get-tuple-element.143), channel_id=1, source_target_pairs={{0,8},{4,12},{8,0},{12,4},{16,24},{20,28},{24,16},{28,20},{1,9},{5... | collective-permute-start | bytes 626696 | tf_op jit(solution)/shard_map/ppermute | solution.py:693
  159.7 5.2 %collective-permute-start.19 = (bf16[1152,384]{1,0:T(8,128)(2,1)S(1)}, bf16[1152,384]{1,0:T(8,128)(2,1)S(1)}, u32[]{:S(2)}, u32[]{:S(2)}) collective-permute-start(bf16[1152,384]{1,0:T(8,128)(2,1)S(1)} %get-tuple-element.161), channel_id=1, source_target_pairs={{0,1},{1,0},{2,3},{3,2},{4,5},{5,4},{6,7},{7,6},{8,9},{9,8},{10,11... | collective-permute-start | bytes 2654216 | tf_op jit(solution)/shard_map/ppermute | solution.py:685
  159.8 3.1 %collective-permute-start.17 = (bf16[288,384]{1,0:T(8,128)(2,1)S(1)}, bf16[288,384]{1,0:T(8,128)(2,1)S(1)}, u32[]{:S(2)}, u32[]{:S(2)}) collective-permute-start(bf16[288,384]{1,0:T(8,128)(2,1)S(1)} %get-tuple-element.158), channel_id=1, source_target_pairs={{0,1},{1,0},{2,3},{3,2},{4,5},{5,4},{6,7},{7,6},{8,9},{9,8},{10,11... | collective-permute-start | bytes 663560 | tf_op jit(solution)/shard_map/ppermute | solution.py:685
  160.3 12.5 %collective-permute-start.23 = (bf16[272,384]{1,0:T(8,128)(2,1)S(1)}, bf16[272,384]{1,0:T(8,128)(2,1)S(1)}, u32[]{:S(2)}, u32[]{:S(2)}) collective-permute-start(bf16[272,384]{1,0:T(8,128)(2,1)S(1)} %fold.20.left), channel_id=1, source_target_pairs={{0,16},{4,20},{8,24},{12,28},{16,0},{20,4},{24,8},{28,12},{1,17},{... | collective-permute-start | bytes 626696 | tf_op jit(solution)/shard_map/ppermute | solution.py:693
  162.9 1.2 collective-permute-start.16
  163.0 8.2 %collective-permute-start.21 = (bf16[288,384]{1,0:T(8,128)(2,1)S(1)}, bf16[288,384]{1,0:T(8,128)(2,1)S(1)}, u32[]{:S(2)}, u32[]{:S(2)}) collective-permute-start(bf16[288,384]{1,0:T(8,128)(2,1)S(1)} %fold.22.left), channel_id=1, source_target_pairs={{0,4},{4,0},{8,12},{12,8},{16,20},{20,16},{24,28},{28,24},{1,5},{5... | collective-permute-start | bytes 663560 | tf_op jit(solution)/shard_map/ppermute | solution.py:693
  164.1 3.8 %collective-permute-start.18 = (f32[16,384]{1,0:T(8,128)S(1)}, f32[16,384]{1,0:T(8,128)S(1)}, u32[]{:S(2)}, u32[]{:S(2)}) collective-permute-start(f32[16,384]{1,0:T(8,128)S(1)} %fold.23.left), channel_id=1, source_target_pairs={{0,2},{2,0},{1,3},{3,1},{4,6},{6,4},{5,7},{7,5},{8,10},{10,8},{9,1... | collective-permute-start | bytes 73736 | tf_op jit(solution)/shard_map/ppermute | solution.py:689
  167.9 19.0 %collective-permute-start.28 = (bf16[576,384]{1,0:T(8,128)(2,1)S(1)}, bf16[576,384]{1,0:T(8,128)(2,1)S(1)}, u32[]{:S(2)}, u32[]{:S(2)}) collective-permute-start(bf16[576,384]{1,0:T(8,128)(2,1)S(1)} %get-tuple-element.174), channel_id=1, source_target_pairs={{0,2},{2,0},{1,3},{3,1},{4,6},{6,4},{5,7},{7,5},{8,10},{10,8},{9,1... | collective-permute-start | bytes 1327112 | tf_op jit(solution)/shard_map/ppermute | solution.py:689
  168.7 3.8 %collective-permute-start.20 = (f32[16,384]{1,0:T(8,128)S(1)}, f32[16,384]{1,0:T(8,128)S(1)}, u32[]{:S(2)}, u32[]{:S(2)}) collective-permute-start(f32[16,384]{1,0:T(8,128)S(1)} %fold.24.left), channel_id=1, source_target_pairs={{0,4},{4,0},{8,12},{12,8},{16,20},{20,16},{24,28},{28,24},{1,5},{5... | collective-permute-start | bytes 73736 | tf_op jit(solution)/shard_map/ppermute | solution.py:693
  171.2 8.4 %collective-permute-start.25 = (bf16[288,384]{1,0:T(8,128)(2,1)S(1)}, bf16[288,384]{1,0:T(8,128)(2,1)S(1)}, u32[]{:S(2)}, u32[]{:S(2)}) collective-permute-start(bf16[288,384]{1,0:T(8,128)(2,1)S(1)} %fold.25.left), channel_id=1, source_target_pairs={{0,8},{4,12},{8,0},{12,4},{16,24},{20,28},{24,16},{28,20},{1,9},{5... | collective-permute-start | bytes 663560 | tf_op jit(solution)/shard_map/ppermute | solution.py:693
  172.9 13.3 %collective-permute-start.24 = (bf16[272,384]{1,0:T(8,128)(2,1)S(1)}, bf16[272,384]{1,0:T(8,128)(2,1)S(1)}, u32[]{:S(2)}, u32[]{:S(2)}) collective-permute-start(bf16[272,384]{1,0:T(8,128)(2,1)S(1)} %fold.27.kept), channel_id=1, source_target_pairs={{0,8},{4,12},{8,0},{12,4},{16,24},{20,28},{24,16},{28,20},{1,9},{5... | collective-permute-start | bytes 626696 | tf_op jit(solution)/shard_map/ppermute | solution.py:693
  173.5 13.3 %collective-permute-start.22 = (f32[16,384]{1,0:T(8,128)S(1)}, f32[16,384]{1,0:T(8,128)S(1)}, u32[]{:S(2)}, u32[]{:S(2)}) collective-permute-start(f32[16,384]{1,0:T(8,128)S(1)} %fold.26.left), channel_id=1, source_target_pairs={{0,8},{4,12},{8,0},{12,4},{16,24},{20,28},{24,16},{28,20},{1,9},{5... | collective-permute-start | bytes 73736 | tf_op jit(solution)/shard_map/ppermute | solution.py:693
  179.7 11.3 %collective-permute-start.27 = (bf16[288,384]{1,0:T(8,128)(2,1)S(1)}, bf16[288,384]{1,0:T(8,128)(2,1)S(1)}, u32[]{:S(2)}, u32[]{:S(2)}) collective-permute-start(bf16[288,384]{1,0:T(8,128)(2,1)S(1)} %fold.28.left), channel_id=1, source_target_pairs={{0,16},{4,20},{8,24},{12,28},{16,0},{20,4},{24,8},{28,12},{1,17},{... | collective-permute-start | bytes 663560 | tf_op jit(solution)/shard_map/ppermute | solution.py:693
  186.2 8.9 %collective-permute-start.29 = (bf16[544,384]{1,0:T(8,128)(2,1)S(1)}, bf16[544,384]{1,0:T(8,128)(2,1)S(1)}, u32[]{:S(2)}, u32[]{:S(2)}) collective-permute-start(bf16[544,384]{1,0:T(8,128)(2,1)S(1)} %join.2.kept), channel_id=1, source_target_pairs={{0,4},{4,0},{8,12},{12,8},{16,20},{20,16},{24,28},{28,24},{1,5},{5... | collective-permute-start | bytes 1253384 | tf_op jit(solution)/shard_map/ppermute | solution.py:693
  186.8 4.8 %collective-permute-start.26 = (f32[16,384]{1,0:T(8,128)S(1)}, f32[16,384]{1,0:T(8,128)S(1)}, u32[]{:S(2)}, u32[]{:S(2)}) collective-permute-start(f32[16,384]{1,0:T(8,128)S(1)} %fold.29.left), channel_id=1, source_target_pairs={{0,16},{4,20},{8,24},{12,28},{16,0},{20,4},{24,8},{28,12},{1,17},{... | collective-permute-start | bytes 73736 | tf_op jit(solution)/shard_map/ppermute | solution.py:693
  195.5 4.3 %collective-permute-start.30 = (bf16[192,384]{1,0:T(8,128)(2,1)S(1)}, bf16[192,384]{1,0:T(8,128)(2,1)S(1)}, u32[]{:S(2)}, u32[]{:S(2)}) collective-permute-start(bf16[192,384]{1,0:T(8,128)(2,1)S(1)} %slice.47), channel_id=1, source_target_pairs={{0,1},{1,0},{2,3},{3,2},{4,5},{5,4},{6,7},{7,6},{8,9},{9,8},{10,11... | collective-permute-start | bytes 442376 | tf_op jit(solution)/shard_map/ppermute | solution.py:685
  (52 other events, 198.4 us)

commit v2 on v1

--- a/solution.py
+++ b/solution.py
@@ -24,7 +24,7 @@
 GELU_B = 0.044715
 SMALL = 16
 BLOCK = 384
-ROWS = 64
+ROWS = 128
 CHUNKS = 3
 
 bf16 = jnp.bfloat16

time: 202 us -> 202 us (level)
  no operation moved by 1% of the time
where the time goes in v2:
time: 202 us; the launch traced here: 201 us
  Pallas kernels  123 us (61%)
  waiting for transfers between devices  28.6 us (14%)
  starting transfers between devices  25.5 us (13%)
  local copies, waits for them, and re-layouts  13.8 us (7%)
  other arithmetic  8.78 us (4%)
    pallas_call x31, Pallas kernels, kernel_call(): pl.pallas_call(body, out_shape=outs, in_specs=in_specs or [VMEM] * len(in...  123 us
    ppermute x11, waiting for transfers between devices, swap_dp(): return lax.ppermute(values, 'dp', [(i, i ^ step) for i in range(size)])  15 us
    ppermute x11, starting transfers between devices, swap_dp(): return lax.ppermute(values, 'dp', [(i, i ^ step) for i in range(size)])  13 us
    unnamed x138, local copies, waits for them, and re-layouts  12.4 us
    ppermute x8, starting transfers between devices, swap_chip(): return lax.ppermute(values, 'tp', CHIP_PAIRS)  10.5 us
    ppermute x8, waiting for transfers between devices, swap_chip(): return lax.ppermute(values, 'tp', CHIP_PAIRS)  9.81 us
    add x6, other arithmetic, update(): average_new = AVERAGE_RATE * average + (1.0 - AVERAGE_RATE) * weight_new  6.53 us
  transfers between devices with their start and end apart: 31, of which 12 were waited for; matrix products, arithmetic and copies ran while one was open for 4% of the time, Pallas kernels for 44%

profile of v2, /device:TPU:0, one launch (start us, length us, event | category | flops | bytes accessed | tf_op | source)
XLA Modules:
  0.0 201.5 jit_solution(14483456967043808221)
XLA Ops:
  0.8 2.1 %take.1 = bf16[576,384]{1,0:T(8,128)(2,1)} custom-call(s32[1]{0:T(128)} %bitcast.1.place, bf16[2,576,384]{2,1,0:T(8,128)(2,1)} %frames.1), custom_call_target="tpu_custom_call" | custom-call | flops 1000000000 | tf_op jit(solution)/shard_map/take/pallas_call | solution.py:38
  2.9 2.9 %collective-permute-start = (bf16[576,384]{1,0:T(8,128)(2,1)}, bf16[576,384]{1,0:T(8,128)(2,1)}, u32[]{:S(2)}, u32[]{:S(2)}) collective-permute-start(bf16[576,384]{1,0:T(8,128)(2,1)} %take.1), channel_id=1, source_target_pairs={{0,2},{2,0},{1,3},{3,1},{4,6},{6,4},{5,7},{7,5},{8,10},{10,8},{9,1... | collective-permute-start | bytes 1327112 | tf_op jit(solution)/shard_map/ppermute | solution.py:689
  6.5 1.6 pack.1
  8.1 8.1 %collective-permute-done.got = bf16[576,384]{1,0:T(8,128)(2,1)} collective-permute-done((bf16[576,384]{1,0:T(8,128)(2,1)}, bf16[576,384]{1,0:T(8,128)(2,1)}, u32[]{:S(2)}, u32[]{:S(2)}) %collective-permute-start) | collective-permute-done | bytes 442400 | tf_op jit(solution)/shard_map/ppermute | solution.py:689
  17.7 1.7 collective-permute-start.4
  20.9 1.0 copy-done.22
  21.9 0.9 copy-done.26
  22.9 3.7 %project_near.1 = (bf16[192,1152]{1,0:T(8,128)(2,1)S(1)}, bf16[192,2304]{1,0:T(8,128)(2,1)S(1)}, bf16[256,2304]{1,0:T(8,128)(2,1)S(1)}, bf16[2304,384]{1,0:T(8,128)(2,1)S(1)}, bf16[2304,384]{1,0:T(8,128)(2,1)S(1)}) custom-call(s32[1]{0:T(128)} %bitcast.place, bf16[2,576,384]{2,1,0:T(8,128)(2,1)} %frames.1, bf16[576,384]{1,0:T(8,128)(2,1)} %collective-permute-done.got, ...), custom_call_target="tpu_custom_call" | custom-call | flops 4000000000 | tf_op jit(solution)/shard_map/project_near/pallas_call | solution.py:38
  27.6 0.8 collective-permute-start.8
  28.3 15.8 %attention_forward.2 = (bf16[192,1152]{1,0:T(8,128)(2,1)S(1)}, f32[4,1152]{1,0:T(4,128)S(1)}, bf16[8,1152,2304]{2,1,0:T(8,128)(2,1)}) custom-call(bf16[192,1152]{1,0:T(8,128)(2,1)S(1)} %get-tuple-element.146.query, bf16[192,2304]{1,0:T(8,128)(2,1)S(1)} %get-tuple-element.104.key, bf16[256,2304]{1,0:T(8,128)(2,1)S(1)} %get-tuple-element.105.value), custom_call_target="tpu_custom_call" | custom-call | flops 16000000000 | tf_op jit(solution)/shard_map/attention_forward/pallas_call | solution.py:38
  44.2 1.4 project_far.1
  45.7 1.3 collective-permute-start.6
  47.1 15.8 %attention_forward.3 = (bf16[192,1152]{1,0:T(8,128)(2,1)S(1)}, f32[4,1152]{1,0:T(4,128)S(1)}, bf16[8,1152,2304]{2,1,0:T(8,128)(2,1)}) custom-call(bf16[192,1152]{1,0:T(8,128)(2,1)S(1)} %get-tuple-element.126.query, bf16[192,2304]{1,0:T(8,128)(2,1)S(1)} %get-tuple-element.112.key, ...), custom_call_target="tpu_custom_call", output_to_operand_aliasing={{2}: (3, {})} | custom-call | flops 16000000000 | tf_op jit(solution)/shard_map/attention_forward/pallas_call | solution.py:38
  63.0 26.0 %middle_step.1 = (f32[1152,384]{1,0:T(8,128)S(1)}, bf16[192,1152]{1,0:T(8,128)(2,1)S(1)}, bf16[192,1152]{1,0:T(8,128)(2,1)S(1)}, bf16[1952,384]{1,0:T(8,128)(2,1...) custom-call(s32[2]{0:T(128)S(1)} %pad_add_fusion.place, ...), custom_call_target="tpu_custom_call" | custom-call | flops 20000000000 | tf_op jit(solution)/shard_map/middle_step/pallas_call | solution.py:38
  89.1 1.1 copy-done
  90.2 1.2 copy-done.34
  91.4 0.8 copy-done.46
  93.3 3.3 %collective-permute-done.10.right = bf16[1952,384]{1,0:T(8,128)(2,1)} collective-permute-done((bf16[1952,384]{1,0:T(8,128)(2,1)}, bf16[1952,384]{1,0:T(8,128)(2,1)}, u32[]{:S(2)}, u32[]{:S(2)}) %collective-permute-start.10) | collective-permute-done | bytes 1499168 | tf_op jit(solution)/shard_map/ppermute | solution.py:685
  96.5 1.4 copy-done.1
  97.9 1.9 fold.16
  99.9 0.9 collective-permute-start.11
  100.8 1.0 copy-done.47
  101.8 22.1 %attention_backward.3 = (bf16[192,1152]{1,0:T(8,128)(2,1)S(1)}, bf16[192,2304]{1,0:T(8,128)(2,1)S(1)}, bf16[192,2304]{1,0:T(8,128)(2,1)S(1)}) custom-call(bf16[192,1152]{1,0:T(8,128)(2,1)S(1)} %copy-done.43, bf16[192,2304]{1,0:T(8,128)(2,1)S(1)} %copy-done.41, bf16[256,2304]{1,0:T(8,128)(2,1)S(1)} %copy-done.39, bf16[192,1152]{1,0:T(8,128)(2,1)S(1)} %copy-done.45, ...), custom_call_target="tpu_custom_call" | custom-call | flops 22000001024 | tf_op jit(solution)/shard_map/attention_backward/pallas_call | solution.py:38
  124.2 1.6 collective-permute-start.12
  125.8 1.3 far_grads.1
  127.2 12.2 %attention_backward.4 = (bf16[96,1152]{1,0:T(8,128)(2,1)S(1)}, bf16[96,2304]{1,0:T(8,128)(2,1)S(1)}, bf16[96,2304]{1,0:T(8,128)(2,1)S(1)}) custom-call(bf16[192,1152]{1,0:T(8,128)(2,1)S(1)} %get-tuple-element.146.query, bf16[192,2304]{1,0:T(8,128)(2,1)S(1)} %get-tuple-element.104.key, bf16[256,2304]{1,0:T(8,128)(2,1)S(1)} %get-tuple-element.105.value, ...), custom_call_target="tpu_custom_call" | custom-call | flops 11000000512 | tf_op jit(solution)/shard_map/attention_backward/pallas_call | solution.py:38
  139.5 1.3 collective-permute-start.15
  141.0 1.6 collective-permute-start.14
  142.6 12.2 %attention_backward.5 = (bf16[96,1152]{1,0:T(8,128)(2,1)S(1)}, bf16[96,2304]{1,0:T(8,128)(2,1)S(1)}, bf16[96,2304]{1,0:T(8,128)(2,1)S(1)}) custom-call(bf16[192,1152]{1,0:T(8,128)(2,1)S(1)} %get-tuple-element.146.query, bf16[192,2304]{1,0:T(8,128)(2,1)S(1)} %get-tuple-element.104.key, bf16[256,2304]{1,0:T(8,128)(2,1)S(1)} %get-tuple-element.105.value, ...), custom_call_target="tpu_custom_call" | custom-call | flops 11000000512 | tf_op jit(solution)/shard_map/attention_backward/pallas_call | solution.py:38
  155.0 4.5 %post_step.1 = (f32[1152,384]{1,0:T(8,128)S(1)}, bf16[1152,384]{1,0:T(8,128)(2,1)S(1)}, bf16[288,384]{1,0:T(8,128)(2,1)S(1)}, bf16[288,384]{1,0:T(8,128)(2,1)S(1)}, f32[16,384]{1,0:T(8,128)S(1)}) custom-call(bf16[96,1152]{1,0:T(8,128)(2,1)S(1)} %get-tuple-element.140.refs_0_, bf16[96,1152]{1,0:T(8,128)(2,1)S(1)} %get-tuple-element.147.refs_1_, ...), custom_call_target="tpu_custom_call" | custom-call | flops 8000000000 | tf_op jit(solution)/shard_map/post_step/pallas_call | solution.py:38
  160.1 2.6 %collective-permute-start.23 = (bf16[272,384]{1,0:T(8,128)(2,1)S(1)}, bf16[272,384]{1,0:T(8,128)(2,1)S(1)}, u32[]{:S(2)}, u32[]{:S(2)}) collective-permute-start(bf16[272,384]{1,0:T(8,128)(2,1)S(1)} %fold.20.left), channel_id=1, source_target_pairs={{0,16},{4,20},{8,24},{12,28},{16,0},{20,4},{24,8},{28,12},{1,17},{... | collective-permute-start | bytes 626696 | tf_op jit(solution)/shard_map/ppermute | solution.py:693
  163.9 0.8 collective-permute-start.18
  164.7 1.4 finish.1
  166.0 1.6 collective-permute-done.18.right
  167.7 0.8 collective-permute-start.28
  168.5 1.1 collective-permute-start.20
  169.6 1.4 collective-permute-done.21.right
  171.0 0.9 collective-permute-start.25
  173.3 1.5 collective-permute-start.22
  174.8 4.7 %collective-permute-done.25.right = bf16[288,384]{1,0:T(8,128)(2,1)S(1)} collective-permute-done((bf16[288,384]{1,0:T(8,128)(2,1)S(1)}, bf16[288,384]{1,0:T(8,128)(2,1)S(1)}, u32[]{:S(2)}, u32[]{:S(2)}) %collective-permute-start.25) | collective-permute-done | bytes 221216 | tf_op jit(solution)/shard_map/ppermute | solution.py:693
  179.5 1.9 collective-permute-start.27
  181.4 4.5 %collective-permute-done.24.got = bf16[272,384]{1,0:T(8,128)(2,1)S(1)} collective-permute-done((bf16[272,384]{1,0:T(8,128)(2,1)S(1)}, bf16[272,384]{1,0:T(8,128)(2,1)S(1)}, u32[]{:S(2)}, u32[]{:S(2)}) %collective-permute-start.24) | collective-permute-done | bytes 208928 | tf_op jit(solution)/shard_map/ppermute | solution.py:693
  186.7 1.3 maximum_select_fusion
  188.1 2.7 %collective-permute-done.27.right = bf16[288,384]{1,0:T(8,128)(2,1)S(1)} collective-permute-done((bf16[288,384]{1,0:T(8,128)(2,1)S(1)}, bf16[288,384]{1,0:T(8,128)(2,1)S(1)}, u32[]{:S(2)}, u32[]{:S(2)}) %collective-permute-start.27) | collective-permute-done | bytes 221216 | tf_op jit(solution)/shard_map/ppermute | solution.py:693
  193.2 1.2 multiply_add_fusion.6
  196.8 1.9 multiply_add_fusion.1
  198.7 0.8 multiply_add_fusion.8
  200.1 1.4 multiply_add_fusion
  (206 shorter events, 15.6 us)
Async XLA Ops:
  2.9 13.4 %collective-permute-start = (bf16[576,384]{1,0:T(8,128)(2,1)}, bf16[576,384]{1,0:T(8,128)(2,1)}, u32[]{:S(2)}, u32[]{:S(2)}) collective-permute-start(bf16[576,384]{1,0:T(8,128)(2,1)} %take.1), channel_id=1, source_target_pairs={{0,2},{2,0},{1,3},{3,1},{4,6},{6,4},{5,7},{7,5},{8,10},{10,8},{9,1... | collective-permute-start | bytes 1327112 | tf_op jit(solution)/shard_map/ppermute | solution.py:689
  5.8 14.3 %collective-permute-start.1 = (bf16[2,576,384]{2,1,0:T(8,128)(2,1)}, bf16[2,576,384]{2,1,0:T(8,128)(2,1)}, u32[]{:S(2)}, u32[]{:S(2)}) collective-permute-start(bf16[2,576,384]{2,1,0:T(8,128)(2,1)} %frames.1), channel_id=1, source_target_pairs={{0,1},{1,0},{2,3},{3,2},{4,5},{5,4},{6,7},{7,6},{8,9},{9,8},{10,11... | collective-permute-start | bytes 2654216 | tf_op jit(solution)/shard_map/ppermute | solution.py:685
  6.5 14.4 %copy-start.13 = (f32[9,384]{1,0:T(8,128)S(1)}, f32[9,384]{1,0:T(8,128)}, u32[]{:S(2)}) copy-start(f32[9,384]{1,0:T(8,128)} %vectors.5) | copy-start | bytes 41476
  8.1 18.4 %copy-start.19 = (bf16[576,384]{1,0:T(8,128)(2,1)}, bf16[576,384]{1,0:T(8,128)(2,1)S(1)}, u32[]{:S(2)}) copy-start(bf16[576,384]{1,0:T(8,128)(2,1)S(1)} %get-tuple-element.118) | copy-start | bytes 1327108
  16.3 3.8 %collective-permute-start.2 = (bf16[576,384]{1,0:T(8,128)(2,1)}, bf16[576,384]{1,0:T(8,128)(2,1)S(1)}, u32[]{:S(2)}, u32[]{:S(2)}) collective-permute-start(bf16[576,384]{1,0:T(8,128)(2,1)} %collective-permute-done.got), channel_id=1, source_target_pairs={{0,1},{1,0},{2,3},{3,2},{4,5},{5,4},{6,7},{7,6},{8,9},{9,8},{10,11... | collective-permute-start | bytes 1327112 | tf_op jit(solution)/shard_map/ppermute | solution.py:685
  16.3 3.2 %collective-permute-start.3 = (bf16[288,384]{1,0:T(8,128)(2,1)S(1)}, bf16[288,384]{1,0:T(8,128)(2,1)S(1)}, u32[]{:S(2)}, u32[]{:S(2)}) collective-permute-start(bf16[288,384]{1,0:T(8,128)(2,1)S(1)} %get-tuple-element.109.left.refs_13_), channel_id=1, source_target_pairs={{0,1},{1,0},{2,3},{3,2},{4,5},{5,4},{6,7},{7,6},{8,9},{9,8},{10,11... | collective-permute-start | bytes 663560 | tf_op jit(solution)/shard_map/ppermute | solution.py:685
  16.8 46.2 %collective-permute-start.7 = (bf16[880,384]{1,0:T(8,128)(2,1)}, bf16[880,384]{1,0:T(8,128)(2,1)}, u32[]{:S(2)}, u32[]{:S(2)}) collective-permute-start(bf16[880,384]{1,0:T(8,128)(2,1)} %get-tuple-element.120.refs_0_), channel_id=1, source_target_pairs={{0,1},{1,0},{2,3},{3,2},{4,5},{5,4},{6,7},{7,6},{8,9},{9,8},{10,11... | collective-permute-start | bytes 2027528 | tf_op jit(solution)/shard_map/ppermute | solution.py:685
  17.7 9.6 %collective-permute-start.4 = (bf16[288,384]{1,0:T(8,128)(2,1)S(1)}, bf16[288,384]{1,0:T(8,128)(2,1)S(1)}, u32[]{:S(2)}, u32[]{:S(2)}) collective-permute-start(bf16[288,384]{1,0:T(8,128)(2,1)S(1)} %get-tuple-element.109.left.refs_13_), channel_id=1, source_target_pairs={{0,2},{2,0},{1,3},{3,1},{4,6},{6,4},{5,7},{7,5},{8,10},{10,8},{9,1... | collective-permute-start | bytes 663560 | tf_op jit(solution)/shard_map/ppermute | solution.py:689
  27.3 16.9 %copy-start.36 = (bf16[2304,384]{1,0:T(8,128)(2,1)}, bf16[2304,384]{1,0:T(8,128)(2,1)S(1)}, u32[]{:S(2)}) copy-start(bf16[2304,384]{1,0:T(8,128)(2,1)S(1)} %get-tuple-element.154.first.refs_9_) | copy-start | bytes 5308420
  27.3 35.8 %copy-start.32 = (bf16[2304,384]{1,0:T(8,128)(2,1)}, bf16[2304,384]{1,0:T(8,128)(2,1)S(1)}, u32[]{:S(2)}) copy-start(bf16[2304,384]{1,0:T(8,128)(2,1)S(1)} %get-tuple-element.116.frames.refs_10_) | copy-start | bytes 5308420
  27.3 16.9 %copy-start.28 = (bf16[288,384]{1,0:T(8,128)(2,1)}, bf16[288,384]{1,0:T(8,128)(2,1)S(1)}, u32[]{:S(2)}) copy-start(bf16[288,384]{1,0:T(8,128)(2,1)S(1)} %collective-permute-done.4.refs_0_.refs_15_) | copy-start | bytes 663556
  27.3 16.9 %collective-permute-start.5 = (bf16[288,384]{1,0:T(8,128)(2,1)S(1)}, bf16[288,384]{1,0:T(8,128)(2,1)S(1)}, u32[]{:S(2)}, u32[]{:S(2)}) collective-permute-start(bf16[288,384]{1,0:T(8,128)(2,1)S(1)} %collective-permute-done.4.refs_0_.refs_15_), channel_id=1, source_target_pairs={{0,1},{1,0},{2,3},{3,2},{4,5},{5,4},{6,7},{7,6},{8,9},{9,8},{10,11... | collective-permute-start | bytes 663560 | tf_op jit(solution)/shard_map/ppermute | solution.py:685
  27.6 19.5 %collective-permute-start.8 = (bf16[880,384]{1,0:T(8,128)(2,1)}, bf16[880,384]{1,0:T(8,128)(2,1)S(1)}, u32[]{:S(2)}, u32[]{:S(2)}) collective-permute-start(bf16[880,384]{1,0:T(8,128)(2,1)} %get-tuple-element.120.refs_0_), channel_id=1, source_target_pairs={{0,2},{2,0},{1,3},{3,1},{4,6},{6,4},{5,7},{7,5},{8,10},{10,8},{9,1... | collective-permute-start | bytes 2027528 | tf_op jit(solution)/shard_map/ppermute | solution.py:689
  45.7 17.2 %copy-start.38 = (bf16[256,2304]{1,0:T(8,128)(2,1)}, bf16[256,2304]{1,0:T(8,128)(2,1)S(1)}, u32[]{:S(2)}) copy-start(bf16[256,2304]{1,0:T(8,128)(2,1)S(1)} %get-tuple-element.113.value) | copy-start | bytes 3538948
  45.7 17.2 %copy-start.40 = (bf16[192,2304]{1,0:T(8,128)(2,1)}, bf16[192,2304]{1,0:T(8,128)(2,1)S(1)}, u32[]{:S(2)}) copy-start(bf16[192,2304]{1,0:T(8,128)(2,1)S(1)} %get-tuple-element.112.key) | copy-start | bytes 2654212
  45.7 17.2 %copy-start.42 = (bf16[192,1152]{1,0:T(8,128)(2,1)}, bf16[192,1152]{1,0:T(8,128)(2,1)S(1)}, u32[]{:S(2)}) copy-start(bf16[192,1152]{1,0:T(8,128)(2,1)S(1)} %get-tuple-element.126.query) | copy-start | bytes 1327108
  45.7 17.3 %collective-permute-start.6 = (bf16[576,384]{1,0:T(8,128)(2,1)S(1)}, bf16[576,384]{1,0:T(8,128)(2,1)S(1)}, u32[]{:S(2)}, u32[]{:S(2)}) collective-permute-start(bf16[576,384]{1,0:T(8,128)(2,1)S(1)} %copy-done.20), channel_id=1, source_target_pairs={{0,2},{2,0},{1,3},{3,1},{4,6},{6,4},{5,7},{7,5},{8,10},{10,8},{9,1... | collective-permute-start | bytes 1327112 | tf_op jit(solution)/shard_map/ppermute | solution.py:689
  47.0 15.9 %collective-permute-start.9 = (bf16[880,384]{1,0:T(8,128)(2,1)S(1)}, bf16[880,384]{1,0:T(8,128)(2,1)S(1)}, u32[]{:S(2)}, u32[]{:S(2)}) collective-permute-start(bf16[880,384]{1,0:T(8,128)(2,1)S(1)} %collective-permute-done.8.refs_2_), channel_id=1, source_target_pairs={{0,1},{1,0},{2,3},{3,2},{4,5},{5,4},{6,7},{7,6},{8,9},{9,8},{10,11... | collective-permute-start | bytes 2027528 | tf_op jit(solution)/shard_map/ppermute | solution.py:685
  47.0 16.0 %copy-start.6 = (f32[384,384]{1,0:T(8,128)S(1)}, f32[384,384]{1,0:T(8,128)}, u32[]{:S(2)}) copy-start(f32[384,384]{1,0:T(8,128)} %head.1) | copy-start | bytes 1769476
  47.1 16.0 %copy-start.14 = (f32[9,384]{1,0:T(8,128)S(1)}, f32[9,384]{1,0:T(8,128)}, u32[]{:S(2)}) copy-start(f32[9,384]{1,0:T(8,128)} %vectors.5) | copy-start | bytes 41476
  47.1 16.0 %copy-start.18 = (bf16[2,576,384]{2,1,0:T(8,128)(2,1)S(1)}, bf16[2,576,384]{2,1,0:T(8,128)(2,1)}, u32[]{:S(2)}) copy-start(bf16[2,576,384]{2,1,0:T(8,128)(2,1)} %targets.3) | copy-start | bytes 2654212
  62.9 26.1 %copy-start.44 = (bf16[192,1152]{1,0:T(8,128)(2,1)}, bf16[192,1152]{1,0:T(8,128)(2,1)S(1)}, u32[]{:S(2)}) copy-start(bf16[192,1152]{1,0:T(8,128)(2,1)S(1)} %get-tuple-element.115.attended_far.mixed) | copy-start | bytes 1327108
  63.0 26.1 %copy-start.48 = (f32[4,1152]{1,0:T(4,128)}, f32[4,1152]{1,0:T(4,128)S(1)}, u32[]{:S(2)}) copy-start(f32[4,1152]{1,0:T(4,128)S(1)} %get-tuple-element.128.totals) | copy-start | bytes 55300
  92.8 3.8 %collective-permute-start.10 = (bf16[1952,384]{1,0:T(8,128)(2,1)}, bf16[1952,384]{1,0:T(8,128)(2,1)}, u32[]{:S(2)}, u32[]{:S(2)}) collective-permute-start(bf16[1952,384]{1,0:T(8,128)(2,1)} %get-tuple-element.123), channel_id=1, source_target_pairs={{0,1},{1,0},{2,3},{3,2},{4,5},{5,4},{6,7},{7,6},{8,9},{9,8},{10,11... | collective-permute-start | bytes 4497416 | tf_op jit(solution)/shard_map/ppermute | solution.py:685
  99.9 24.0 %collective-permute-start.11 = (bf16[1088,384]{1,0:T(8,128)(2,1)S(1)}, bf16[1088,384]{1,0:T(8,128)(2,1)S(1)}, u32[]{:S(2)}, u32[]{:S(2)}) collective-permute-start(bf16[1088,384]{1,0:T(8,128)(2,1)S(1)} %get-tuple-element.125), channel_id=1, source_target_pairs={{0,2},{2,0},{1,3},{3,1},{4,6},{6,4},{5,7},{7,5},{8,10},{10,8},{9,1... | collective-permute-start | bytes 2506760 | tf_op jit(solution)/shard_map/ppermute | solution.py:689
  101.8 24.0 %copy-start.37 = (bf16[2304,384]{1,0:T(8,128)(2,1)S(1)}, bf16[2304,384]{1,0:T(8,128)(2,1)}, u32[]{:S(2)}) copy-start(bf16[2304,384]{1,0:T(8,128)(2,1)} %copy-done.36) | copy-start | bytes 5308420
  124.2 16.6 %collective-permute-start.12 = (bf16[544,384]{1,0:T(8,128)(2,1)S(1)}, bf16[544,384]{1,0:T(8,128)(2,1)S(1)}, u32[]{:S(2)}, u32[]{:S(2)}) collective-permute-start(bf16[544,384]{1,0:T(8,128)(2,1)S(1)} %get-tuple-element.132), channel_id=1, source_target_pairs={{0,4},{4,0},{8,12},{12,8},{16,20},{20,16},{24,28},{28,24},{1,5},{5... | collective-permute-start | bytes 1253384 | tf_op jit(solution)/shard_map/ppermute | solution.py:693
  127.1 12.3 %collective-permute-start.13 = (bf16[288,384]{1,0:T(8,128)(2,1)S(1)}, bf16[288,384]{1,0:T(8,128)(2,1)S(1)}, u32[]{:S(2)}, u32[]{:S(2)}) collective-permute-start(bf16[288,384]{1,0:T(8,128)(2,1)S(1)} %get-tuple-element.136), channel_id=1, source_target_pairs={{0,1},{1,0},{2,3},{3,2},{4,5},{5,4},{6,7},{7,6},{8,9},{9,8},{10,11... | collective-permute-start | bytes 663560 | tf_op jit(solution)/shard_map/ppermute | solution.py:685
  139.5 15.5 %collective-permute-start.15 = (bf16[288,384]{1,0:T(8,128)(2,1)S(1)}, bf16[288,384]{1,0:T(8,128)(2,1)S(1)}, u32[]{:S(2)}, u32[]{:S(2)}) collective-permute-start(bf16[288,384]{1,0:T(8,128)(2,1)S(1)} %fold.19), channel_id=1, source_target_pairs={{0,2},{2,0},{1,3},{3,1},{4,6},{6,4},{5,7},{7,5},{8,10},{10,8},{9,1... | collective-permute-start | bytes 663560 | tf_op jit(solution)/shard_map/ppermute | solution.py:689
  140.9 14.1 %copy-start.15 = (f32[9,384]{1,0:T(8,128)S(1)}, f32[9,384]{1,0:T(8,128)}, u32[]{:S(2)}) copy-start(f32[9,384]{1,0:T(8,128)} %vectors.5) | copy-start | bytes 41476
  140.9 14.1 %copy-start.24 = (bf16[288,384]{1,0:T(8,128)(2,1)S(1)}, bf16[288,384]{1,0:T(8,128)(2,1)}, u32[]{:S(2)}) copy-start(bf16[288,384]{1,0:T(8,128)(2,1)} %copy-done.23) | copy-start | bytes 663556
  140.9 14.0 %copy-start.27 = (bf16[288,384]{1,0:T(8,128)(2,1)S(1)}, bf16[288,384]{1,0:T(8,128)(2,1)}, u32[]{:S(2)}) copy-start(bf16[288,384]{1,0:T(8,128)(2,1)} %copy-done.25) | copy-start | bytes 663556
  141.0 13.9 %collective-permute-start.14 = (bf16[272,384]{1,0:T(8,128)(2,1)S(1)}, bf16[272,384]{1,0:T(8,128)(2,1)S(1)}, u32[]{:S(2)}, u32[]{:S(2)}) collective-permute-start(bf16[272,384]{1,0:T(8,128)(2,1)S(1)} %get-tuple-element.143), channel_id=1, source_target_pairs={{0,8},{4,12},{8,0},{12,4},{16,24},{20,28},{24,16},{28,20},{1,9},{5... | collective-permute-start | bytes 626696 | tf_op jit(solution)/shard_map/ppermute | solution.py:693
  159.5 5.2 %collective-permute-start.19 = (bf16[1152,384]{1,0:T(8,128)(2,1)S(1)}, bf16[1152,384]{1,0:T(8,128)(2,1)S(1)}, u32[]{:S(2)}, u32[]{:S(2)}) collective-permute-start(bf16[1152,384]{1,0:T(8,128)(2,1)S(1)} %get-tuple-element.161), channel_id=1, source_target_pairs={{0,1},{1,0},{2,3},{3,2},{4,5},{5,4},{6,7},{7,6},{8,9},{9,8},{10,11... | collective-permute-start | bytes 2654216 | tf_op jit(solution)/shard_map/ppermute | solution.py:685
  159.6 3.1 %collective-permute-start.17 = (bf16[288,384]{1,0:T(8,128)(2,1)S(1)}, bf16[288,384]{1,0:T(8,128)(2,1)S(1)}, u32[]{:S(2)}, u32[]{:S(2)}) collective-permute-start(bf16[288,384]{1,0:T(8,128)(2,1)S(1)} %get-tuple-element.158), channel_id=1, source_target_pairs={{0,1},{1,0},{2,3},{3,2},{4,5},{5,4},{6,7},{7,6},{8,9},{9,8},{10,11... | collective-permute-start | bytes 663560 | tf_op jit(solution)/shard_map/ppermute | solution.py:685
  160.1 12.5 %collective-permute-start.23 = (bf16[272,384]{1,0:T(8,128)(2,1)S(1)}, bf16[272,384]{1,0:T(8,128)(2,1)S(1)}, u32[]{:S(2)}, u32[]{:S(2)}) collective-permute-start(bf16[272,384]{1,0:T(8,128)(2,1)S(1)} %fold.20.left), channel_id=1, source_target_pairs={{0,16},{4,20},{8,24},{12,28},{16,0},{20,4},{24,8},{28,12},{1,17},{... | collective-permute-start | bytes 626696 | tf_op jit(solution)/shard_map/ppermute | solution.py:693
  162.7 1.2 collective-permute-start.16
  162.8 8.2 %collective-permute-start.21 = (bf16[288,384]{1,0:T(8,128)(2,1)S(1)}, bf16[288,384]{1,0:T(8,128)(2,1)S(1)}, u32[]{:S(2)}, u32[]{:S(2)}) collective-permute-start(bf16[288,384]{1,0:T(8,128)(2,1)S(1)} %fold.22.left), channel_id=1, source_target_pairs={{0,4},{4,0},{8,12},{12,8},{16,20},{20,16},{24,28},{28,24},{1,5},{5... | collective-permute-start | bytes 663560 | tf_op jit(solution)/shard_map/ppermute | solution.py:693
  163.9 3.8 %collective-permute-start.18 = (f32[16,384]{1,0:T(8,128)S(1)}, f32[16,384]{1,0:T(8,128)S(1)}, u32[]{:S(2)}, u32[]{:S(2)}) collective-permute-start(f32[16,384]{1,0:T(8,128)S(1)} %fold.23.left), channel_id=1, source_target_pairs={{0,2},{2,0},{1,3},{3,1},{4,6},{6,4},{5,7},{7,5},{8,10},{10,8},{9,1... | collective-permute-start | bytes 73736 | tf_op jit(solution)/shard_map/ppermute | solution.py:689
  167.7 19.0 %collective-permute-start.28 = (bf16[576,384]{1,0:T(8,128)(2,1)S(1)}, bf16[576,384]{1,0:T(8,128)(2,1)S(1)}, u32[]{:S(2)}, u32[]{:S(2)}) collective-permute-start(bf16[576,384]{1,0:T(8,128)(2,1)S(1)} %get-tuple-element.174), channel_id=1, source_target_pairs={{0,2},{2,0},{1,3},{3,1},{4,6},{6,4},{5,7},{7,5},{8,10},{10,8},{9,1... | collective-permute-start | bytes 1327112 | tf_op jit(solution)/shard_map/ppermute | solution.py:689
  168.5 3.8 %collective-permute-start.20 = (f32[16,384]{1,0:T(8,128)S(1)}, f32[16,384]{1,0:T(8,128)S(1)}, u32[]{:S(2)}, u32[]{:S(2)}) collective-permute-start(f32[16,384]{1,0:T(8,128)S(1)} %fold.24.left), channel_id=1, source_target_pairs={{0,4},{4,0},{8,12},{12,8},{16,20},{20,16},{24,28},{28,24},{1,5},{5... | collective-permute-start | bytes 73736 | tf_op jit(solution)/shard_map/ppermute | solution.py:693
  171.0 8.4 %collective-permute-start.25 = (bf16[288,384]{1,0:T(8,128)(2,1)S(1)}, bf16[288,384]{1,0:T(8,128)(2,1)S(1)}, u32[]{:S(2)}, u32[]{:S(2)}) collective-permute-start(bf16[288,384]{1,0:T(8,128)(2,1)S(1)} %fold.25.left), channel_id=1, source_target_pairs={{0,8},{4,12},{8,0},{12,4},{16,24},{20,28},{24,16},{28,20},{1,9},{5... | collective-permute-start | bytes 663560 | tf_op jit(solution)/shard_map/ppermute | solution.py:693
  172.7 13.3 %collective-permute-start.24 = (bf16[272,384]{1,0:T(8,128)(2,1)S(1)}, bf16[272,384]{1,0:T(8,128)(2,1)S(1)}, u32[]{:S(2)}, u32[]{:S(2)}) collective-permute-start(bf16[272,384]{1,0:T(8,128)(2,1)S(1)} %fold.27.kept), channel_id=1, source_target_pairs={{0,8},{4,12},{8,0},{12,4},{16,24},{20,28},{24,16},{28,20},{1,9},{5... | collective-permute-start | bytes 626696 | tf_op jit(solution)/shard_map/ppermute | solution.py:693
  173.3 13.3 %collective-permute-start.22 = (f32[16,384]{1,0:T(8,128)S(1)}, f32[16,384]{1,0:T(8,128)S(1)}, u32[]{:S(2)}, u32[]{:S(2)}) collective-permute-start(f32[16,384]{1,0:T(8,128)S(1)} %fold.26.left), channel_id=1, source_target_pairs={{0,8},{4,12},{8,0},{12,4},{16,24},{20,28},{24,16},{28,20},{1,9},{5... | collective-permute-start | bytes 73736 | tf_op jit(solution)/shard_map/ppermute | solution.py:693
  179.5 11.3 %collective-permute-start.27 = (bf16[288,384]{1,0:T(8,128)(2,1)S(1)}, bf16[288,384]{1,0:T(8,128)(2,1)S(1)}, u32[]{:S(2)}, u32[]{:S(2)}) collective-permute-start(bf16[288,384]{1,0:T(8,128)(2,1)S(1)} %fold.28.left), channel_id=1, source_target_pairs={{0,16},{4,20},{8,24},{12,28},{16,0},{20,4},{24,8},{28,12},{1,17},{... | collective-permute-start | bytes 663560 | tf_op jit(solution)/shard_map/ppermute | solution.py:693
  186.0 8.9 %collective-permute-start.29 = (bf16[544,384]{1,0:T(8,128)(2,1)S(1)}, bf16[544,384]{1,0:T(8,128)(2,1)S(1)}, u32[]{:S(2)}, u32[]{:S(2)}) collective-permute-start(bf16[544,384]{1,0:T(8,128)(2,1)S(1)} %join.2.kept), channel_id=1, source_target_pairs={{0,4},{4,0},{8,12},{12,8},{16,20},{20,16},{24,28},{28,24},{1,5},{5... | collective-permute-start | bytes 1253384 | tf_op jit(solution)/shard_map/ppermute | solution.py:693
  186.6 4.8 %collective-permute-start.26 = (f32[16,384]{1,0:T(8,128)S(1)}, f32[16,384]{1,0:T(8,128)S(1)}, u32[]{:S(2)}, u32[]{:S(2)}) collective-permute-start(f32[16,384]{1,0:T(8,128)S(1)} %fold.29.left), channel_id=1, source_target_pairs={{0,16},{4,20},{8,24},{12,28},{16,0},{20,4},{24,8},{28,12},{1,17},{... | collective-permute-start | bytes 73736 | tf_op jit(solution)/shard_map/ppermute | solution.py:693
  195.2 4.3 %collective-permute-start.30 = (bf16[192,384]{1,0:T(8,128)(2,1)S(1)}, bf16[192,384]{1,0:T(8,128)(2,1)S(1)}, u32[]{:S(2)}, u32[]{:S(2)}) collective-permute-start(bf16[192,384]{1,0:T(8,128)(2,1)S(1)} %slice.47), channel_id=1, source_target_pairs={{0,1},{1,0},{2,3},{3,2},{4,5},{5,4},{6,7},{7,6},{8,9},{9,8},{10,11... | collective-permute-start | bytes 442376 | tf_op jit(solution)/shard_map/ppermute | solution.py:685
  (52 other events, 198.4 us)
